TPU v7x, 256 devices: a whole 4x4x8 slice. The times are simulated.
256 devices in a mesh: tile: 64 (over z, x, core), rot: 4 (over y).
Axes of the slice: x: 4, y: 4, z: 8, core: 2. Of those that a mesh axis runs over, the one named last changes fastest.
Arguments:
- tomogram: bfloat16 [2048, 5120], P('tile'), may hold values from -12 to 12
- templates: bfloat16 [16, 110592], P('rot', 'tile'), may hold values from -6 to 6
- valid: int32 [2048, 80], P('tile'), may hold values from 0 to 1, as said below
- quats: float32 [4, 4096], replicated, may hold values from -1 to 1, as said below
- rot_index: int32 [16], P('rot'), may hold values from 0 to 4095
Outputs:
- best: float32 [2048, 5120], P('tile', 'rot')
- evidence: float32 [2048, 5120], P('tile', 'rot')
- moments: float32 [4, 2048, 5120], P(None, 'tile', 'rot')
Inputs may be any that keep to these rules, and one draw needn't show every extreme that they name: `valid`: 1 marks a column (x, y) of voxels inside the lamella. `quats`: each column is a unit quaternion with a non-negative first component.
All inputs are finite; a program needn't handle non-finite values.
Results may differ from a plain program's by a relative error of at most 0.0003.
Values may be sent and summed in bfloat16 or wider, within the bound.
A program may use at most 128 MiB of HBM per device.

v0:
```python
import math

import jax
import jax.numpy as jnp
from jax import lax
from jax.sharding import PartitionSpec as P

TEMPL = 48
HALF = 24


EPSILON = 1e-06
TWO_PI = 2.0 * math.pi


def padded(block, sides, width):
    for axis, dim in sides:
        count = lax.axis_size(axis)
        forward = [(i, i + 1) for i in range(count - 1)]
        backward = [(target, source) for source, target in forward]
        low = lax.ppermute(
            lax.slice_in_dim(block, block.shape[dim] - width, None, axis=dim), axis, forward
        )
        high = lax.ppermute(lax.slice_in_dim(block, 0, width, axis=dim), axis, backward)
        block = jnp.concatenate([low, block, high], axis=dim)
    return block


def twiddle(count_in, shift_in, count_out, shift_out, length, direction, factor):
    row_idx = (jnp.arange(count_in, dtype=jnp.int32) + shift_in)[:, None]
    col_idx = (jnp.arange(count_out, dtype=jnp.int32) + shift_out)[None, :]
    phase_idx = jnp.remainder(row_idx * col_idx, length).astype(jnp.float32)
    angles = phase_idx * jnp.float32(direction * TWO_PI / length)
    real_part = jnp.cos(angles) * factor
    imag_part = jnp.sin(angles) * factor
    upper_half = jnp.stack([real_part, imag_part], axis=1)
    lower_half = jnp.stack([-imag_part, real_part], axis=1)
    return jnp.stack([upper_half, lower_half], axis=0)


def product(formula, left_arr, right_arr):
    return jnp.einsum(
        formula,
        left_arr,
        right_arr,
        precision=lax.Precision.HIGH,
        preferred_element_type=jnp.float32,
    )


def forward(volume, shift, direction, lengths):
    size_x, size_y, size_z = volume.shape
    table_z = twiddle(size_z, shift, lengths[2], 0, lengths[2], direction, 1.0)[0]
    spectrum = product("xyz,zdk->dxyk", volume, table_z)
    spectrum = product(
        "cxyz,cydk->dxkz",
        spectrum,
        twiddle(size_y, shift, lengths[1], 0, lengths[1], direction, 1.0),
    )
    return product(
        "cxyz,cxdk->dkyz",
        spectrum,
        twiddle(size_x, shift, lengths[0], 0, lengths[0], direction, 1.0),
    )


def inverse(spectrum, out_x, out_y, out_z, lengths):
    spectrum = product(
        "cxyz,cxdk->dkyz",
        spectrum,
        twiddle(lengths[0], 0, out_x, HALF, lengths[0], 1, 1.0 / lengths[0]),
    )
    spectrum = product(
        "cxyz,cydk->dxkz",
        spectrum,
        twiddle(lengths[1], 0, out_y, 0, lengths[1], 1, 1.0 / lengths[1]),
    )
    real_table = twiddle(lengths[2], 0, out_z, 0, lengths[2], 1, 1.0 / lengths[2])[:, :, 0]
    return product("cxyz,czk->xyk", spectrum, real_table)


def multiply(first_arr, other_arr):
    return jnp.stack(
        [
            first_arr[0] * other_arr[0] - first_arr[1] * other_arr[1],
            first_arr[0] * other_arr[1] + first_arr[1] * other_arr[0],
        ]
    )


def local(tomogram, templates, valid, quats, rot_index):
    x_cells, voxels = tomogram.shape
    y_cells = valid.shape[1]
    z_cells = voxels // y_cells
    lengths = (x_cells + TEMPL, y_cells + HALF, z_cells + HALF)
    widened = padded(tomogram, (("tile", 0),), HALF)
    slab_spectrum = forward(
        widened.astype(jnp.float32).reshape(x_cells + TEMPL, y_cells, z_cells), 0, -1, lengths
    )
    gathered_bank = lax.all_gather(templates, "tile", axis=1, tiled=True).astype(jnp.float32)
    centred = gathered_bank - jnp.mean(gathered_bank, axis=1, keepdims=True)
    tmpl_spread = jnp.sqrt(jnp.mean(centred * centred, axis=1, keepdims=True) + EPSILON)
    unit_bank = centred / (tmpl_spread * jnp.float32(TEMPL) ** 1.5)

    def correlate(unit_tmpl):
        tmpl_spectrum = forward(unit_tmpl.reshape(TEMPL, TEMPL, TEMPL), -HALF, 1, lengths)
        return inverse(multiply(slab_spectrum, tmpl_spectrum), x_cells, y_cells, z_cells, lengths)

    correlation = lax.map(correlate, unit_bank).reshape(unit_bank.shape[0], x_cells, voxels)
    inside = jnp.repeat(valid.astype(jnp.float32), z_cells, axis=1)
    columns = jnp.sum(valid.astype(jnp.float32))
    masked = correlation * inside[None]
    first_sum, all_columns = lax.psum((jnp.sum(masked, axis=(1, 2)), columns), "tile")
    voxel_count = all_columns * z_cells
    average = first_sum / voxel_count
    deviation = correlation - average[:, None, None]
    square_sum = lax.psum(jnp.sum(inside[None] * deviation * deviation, axis=(1, 2)), "tile")
    spread = jnp.sqrt(square_sum / voxel_count + EPSILON)
    scores = (correlation - average[:, None, None]) / spread[:, None, None]
    one_hot = (rot_index[:, None] == jnp.arange(quats.shape[1], dtype=jnp.int32)[None, :]).astype(
        jnp.float32
    )
    orient = product("rq,kq->rk", one_hot, quats)
    highest = jnp.max(scores, axis=0)
    weight = jnp.exp(scores - highest[None])
    exp_total = jnp.sum(weight, axis=0)
    moment = product("rxv,rk->kxv", weight, orient)
    groups = lax.axis_size("rot")
    share_len = voxels // groups
    offset = lax.axis_index("rot") * share_len
    high_full = lax.pmax(highest, "rot")
    rescale = jnp.exp(highest - high_full)
    total_full, moment_full = lax.psum((exp_total * rescale, moment * rescale[None]), "rot")
    high_all = lax.dynamic_slice_in_dim(high_full, offset, share_len, 1)
    total_all = lax.dynamic_slice_in_dim(total_full, offset, share_len, 1)
    moment_all = lax.dynamic_slice_in_dim(moment_full, offset, share_len, 2)
    inside_part = lax.dynamic_slice_in_dim(inside, offset, share_len, 1)
    best = inside_part * high_all
    evidence = inside_part * (high_all + jnp.log(total_all))
    moments = inside_part[None] * moment_all / total_all[None]
    return (best, evidence, moments)


def solution(mesh):
    placed = (P("tile", None), P("rot", "tile"), P("tile", None), P(), P("rot"))
    return jax.shard_map(
        local,
        mesh=mesh,
        in_specs=placed,
        out_specs=(P("tile", "rot"), P("tile", "rot"), P(None, "tile", "rot")),
        check_vma=False,
    )
```

profile of v0, /device:TPU:1, one launch (start us, length us, event | category | flops | bytes accessed | tf_op | source)
XLA Modules:
  0.0 682.8 jit_solution(3317119279552520776)
XLA Ops:
  7.2 1.8 fusion.124
  9.0 4.5 collective-permute-start
  13.5 1.9 collective-permute-start.1
  16.4 55.7 %all-gather = bf16[64,1728,4]{1,2,0:T(4,128)(2,1)S(1)} all-gather(bf16[1,1728,4]{1,2,0:T(4,128)(2,1)} %bitcast.196), channel_id=1, replica_groups=mesh['tile'=64,'rot'=4] {'tile'}, dimensions={0}, use_global_device_ids=true | all-gather | bytes 898560 | tf_op jit(solution)/shard_map/all_gather | solution.py:100
  74.6 2.8 reshape.771
  78.5 1.6 divide_bitcast_fusion
  83.9 4.6 convolution_bitcast_fusion.1
  88.5 9.4 %copy.71 = f32[2,80,80,88,1]{2,1,0,4,3:T(8,128)} copy(f32[2,80,80,88,1]{3,2,1,0,4:T(8,128)} %convolution_bitcast_fusion.1) | data formatting | bytes 9011200 | tf_op jit(solution)/shard_map/xyz,zdk->dxyk/transpose | solution.py:42
  97.9 5.5 fusion.90
  103.4 5.6 fusion.83
  109.0 145.5 %while.13 = (s32[]{:T(128)}, f32[4,32,80,64]{2,3,1,0:T(8,128)}, f32[2,80,104,88]{2,1,3,0:T(8,128)}, f32[4,110592]{1,0:T(4,128)}, s32[]{:T(128)}) while((s32[]{:T(128)}, f32[4,32,80,64]{2,3,1,0:T(8,128)}, f32[2,80,104,88]{2,1,3,0:T(8,128)}, f32[4,110592]{1,0:T(4,128)}, s32[]{:T(128)}) %tuple.86), condition=%wide.region_3.4_spmd, body=%wide.region_2.3_spmd.sunk | while | flops 2770436608 | bytes 55842368 | solution.py:109
  109.6 2.8 dynamic-slice_reduce_fusion.2
  114.1 2.3 convolution_bitcast_fusion.4
  116.4 4.6 copy.104
  121.0 3.8 fusion.158
  125.0 3.1 fusion.160
  128.1 5.9 multiply_subtract_fusion.2
  134.2 4.5 fusion.161
  139.1 3.5 fusion.163
  142.9 2.7 fusion.165
  145.9 2.8 dynamic-slice_reduce_fusion.2
  148.6 1.5 reshape.806
  150.3 2.3 convolution_bitcast_fusion.4
  152.6 4.6 copy.104
  157.2 3.8 fusion.158
  161.3 3.1 fusion.160
  164.3 5.9 multiply_subtract_fusion.2
  170.4 4.5 fusion.161
  175.3 3.5 fusion.163
  179.2 2.7 fusion.165
  182.1 2.8 dynamic-slice_reduce_fusion.2
  184.9 1.5 reshape.806
  186.5 2.3 convolution_bitcast_fusion.4
  188.9 4.6 copy.104
  193.5 3.8 fusion.158
  197.5 3.1 fusion.160
  200.6 5.9 multiply_subtract_fusion.2
  206.7 4.5 fusion.161
  211.6 3.5 fusion.163
  215.4 2.7 fusion.165
  218.3 2.8 dynamic-slice_reduce_fusion.2
  221.1 1.5 reshape.806
  222.8 2.3 convolution_bitcast_fusion.4
  225.1 4.6 copy.104
  229.7 3.8 fusion.158
  233.7 3.1 fusion.160
  236.8 5.9 multiply_subtract_fusion.2
  242.9 4.5 fusion.161
  247.8 3.5 fusion.163
  251.6 2.7 fusion.165
  254.5 2.8 multiply_reduce_fusion
  257.6 124.2 %all-reduce = (f32[4]{0:T(128)S(1)}, f32[]{:T(128)}) all-reduce(f32[4]{0:T(128)S(1)} %multiply_reduce_fusion, f32[]{:T(128)} %convert_reduce_fusion.1), channel_id=1, replica_groups=mesh['tile'=64,'rot'=4] {'tile'}, use_global_device_ids=true, to_apply=%region_5.6 | all-reduce | flops 5 | bytes 40 | tf_op jit(solution)/shard_map/psum | solution.py:113
  382.5 3.1 fusion.82
  385.6 5.7 copy.55
  391.3 126.7 %psum.37 = f32[4]{0:T(128)S(1)} all-reduce(f32[4]{0:T(128)S(1)} %fusion.82), channel_id=1, replica_groups=mesh['tile'=64,'rot'=4] {'tile'}, use_global_device_ids=true, to_apply=%region_9.10 | all-reduce | flops 4 | bytes 32 | tf_op jit(solution)/shard_map/psum | solution.py:117
  518.0 3.0 fusion.122
  521.4 4.4 exponential_reduce_fusion
  527.0 5.4 reshape.768
  534.2 2.2 subtract_exponential_fusion
  536.4 41.4 %all-reduce.5.cloned.1.call-done = f32[32,5120]{1,0:T(8,128)} async-done(((f32[32,5120]{1,0:T(8,128)}), f32[32,5120]{1,0:T(8,128)}) %all-reduce.5.cloned.1.call-update) | async-done | bytes 655376 | tf_op jit(solution)/shard_map/pmax | solution.py:131
  577.8 2.2 fusion.123
  580.0 5.6 convolution_multiply_fusion
  586.5 85.2 %all-reduce.7.cloned.1.call-done = (f32[32,5120]{1,0:T(8,128)}, f32[4,32,5120]{2,0,1:T(4,128)}) async-done(((f32[32,5120]{1,0:T(8,128)}, f32[4,32,5120]{2,0,1:T(4,128)}), (f32[32,5120]{1,0:T(8,128)}, f32[4,32,5120]{2,0,1:T(4,128)})) %all-reduce.7.cloned.1.call-update) | async-done | bytes 3276816 | tf_op jit(solution)/shard_map/psum | solution.py:133
  671.7 1.8 add_multiply_fusion
  (109 shorter events, 22.2 us)
Async XLA Ops:
  7.2 250.2 %copy-start = (f32[4,4096]{1,0:T(4,128)S(1)}, f32[4,4096]{1,0:T(4,128)}, u32[]{:S(2)}) copy-start(f32[4,4096]{1,0:T(4,128)} %param.10) | copy-start | bytes 196612
  7.2 570.6 %all-reduce.5.cloned.1.call-start = ((), (), s32[]{:S(2)}) async-start(), calls=%async_computation | async-start | bytes 1310720 | tf_op jit(solution)/shard_map/pmax | solution.py:131
  9.0 71.8 %collective-permute-start = (bf16[24,5120]{1,0:T(8,128)(2,1)}, bf16[24,5120]{1,0:T(8,128)(2,1)S(1)}, u32[]{:S(2)}, u32[]{:S(2)}) collective-permute-start(bf16[24,5120]{1,0:T(8,128)(2,1)} %get-tuple-element.138), channel_id=1, source_target_pairs={{0,4},{4,8},{8,12},{12,16},{16,20},{20,24},{24,28},{28,32},{32,36}... | collective-permute-start | bytes 737288 | tf_op jit(solution)/shard_map/ppermute | solution.py:21
  13.5 68.0 %collective-permute-start.1 = (bf16[24,5120]{1,0:T(8,128)(2,1)S(1)}, bf16[24,5120]{1,0:T(8,128)(2,1)}, u32[]{:S(2)}, u32[]{:S(2)}) collective-permute-start(bf16[24,5120]{1,0:T(8,128)(2,1)S(1)} %get-tuple-element.139), channel_id=1, source_target_pairs={{4,0},{8,4},{12,8},{16,12},{20,16},{24,20},{28,24},{32,28},{36,32}... | collective-permute-start | bytes 737288 | tf_op jit(solution)/shard_map/ppermute | solution.py:24
  74.6 5.6 copy-start.5
  77.4 4.1 copy-start.3
  80.8 0.7 copy-start.4
  254.5 2.9 copy-start.6
  527.0 5.4 copy-start.2
  532.5 1.7 copy-start.1
  534.1 137.6 %all-reduce.7.cloned.1.call-start = ((), (), s32[]{:S(2)}) async-start(), calls=%async_computation.1 | async-start | bytes 6553600 | tf_op jit(solution)/shard_map/psum | solution.py:133
Sparse Core Ops, SparseCore 0:
  534.2 43.5 all-reduce.4
  585.8 85.7 all-reduce.6
where the time goes:
time: 690 us; the launch traced here: 683 us
  blocking collectives  307 us (44%)
  waiting for transfers between devices  127 us (18%)
  matrix products  101 us (15%)
  local copies, waits for them, and re-layouts  68.8 us (10%)
  other arithmetic  56.8 us (8%)
  between operations  15.1 us (2%)
    psum x1, blocking collectives, local(): lax.psum(jnp.sum(inside[None] * deviation * deviation, axis=(1, 2)), 'tile')  127 us
    psum x1, blocking collectives, local(): lax.psum((jnp.sum(masked, axis=(1, 2)), columns), 'tile')  124 us
    dot_general x29, matrix products, product(): jnp.einsum(formula, left_arr, right_arr, precision=lax.Precision.HIGH, pr...  101 us
    psum x1, waiting for transfers between devices, local(): lax.psum((exp_total * rescale, moment * rescale[None]), 'rot')  85.2 us
    all_gather x1, blocking collectives, local(): lax.all_gather(templates, 'tile', axis=1, tiled=True).astype(jnp.float32)  55.7 us
    pmax x1, waiting for transfers between devices, local(): high_full = lax.pmax(highest, 'rot')  41.4 us
    transpose x5, local copies, waits for them, and re-layouts, product(): jnp.einsum(formula, left_arr, right_arr, precision=lax.Precision.HIGH, pr...  27.7 us
    sub x4, other arithmetic, multiply(): first_arr[0] * other_arr[0] - first_arr[1] * other_arr[1]  23.7 us
  transfers between devices with their start and end apart: 4, of which 2 were waited for; matrix products, arithmetic and copies ran while one was open for 2% of the time, Pallas kernels for 0%

commit v1 on v0

v1 whole, which is shorter than its diff:
```python
import functools
import math

import jax
import jax.numpy as jnp
import ml_dtypes
import numpy as np
from jax import lax
from jax.experimental import pallas as pl
from jax.experimental.pallas import tpu as pltpu
from jax.sharding import PartitionSpec as P

TEMPL = 48
HALF = 24
EPSILON = 1e-06
LANES = 128
ZF = 64
F32 = jnp.float32
BF16 = jnp.bfloat16


def halves(table):
    high = table.astype(np.float32).astype(ml_dtypes.bfloat16)
    low = (table - high.astype(np.float64)).astype(np.float32).astype(ml_dtypes.bfloat16)
    return high, low


def row_tables(table):
    high, low = halves(table)
    return np.concatenate([high, low], axis=0)


def col_tables(table):
    high, low = halves(table)
    return np.concatenate([high, low], axis=1)


def phases(rows, cols, length):
    index = np.outer(np.asarray(rows), np.asarray(cols)) % length
    return index * (2.0 * np.pi / length)


def padded_rows(table, rows):
    return np.pad(table, ((0, rows - table.shape[0]), (0, 0)))


def padded_cols(table, cols):
    return np.pad(table, ((0, 0), (0, cols - table.shape[1])))


def up8(n):
    return -(-n // 8) * 8


class Plan:
    def __init__(self, xs, ys, zs):
        self.xs, self.ys, self.zs = xs, ys, zs
        self.lx, self.ly, self.lz = xs + TEMPL, ys + HALF, zs + HALF
        self.kx, self.ky, self.kz = self.lx // 2 + 1, self.ly // 2 + 1, self.lz // 2 + 1
        self.kxp, self.kyp = up8(self.kx), up8(self.ky)
        self.kxi = up8(2 * self.kx)

    def folded(self, count, pad, points, length):
        angle = phases(np.arange(count), points, length)
        return np.concatenate(
            [padded_rows(np.cos(angle), pad), padded_rows(np.sin(angle), pad)], axis=0
        )

    def slab_z(self):
        angle = phases(np.arange(self.zs), np.arange(self.kz), self.lz)
        cos = padded_cols(np.cos(angle), ZF)
        sin = padded_cols(-np.sin(angle), ZF)
        one = np.concatenate([cos, cos, sin, sin], axis=1)
        none = np.zeros_like(one)
        high, low = halves(np.block([[one, none], [none, one]]))
        return np.concatenate([high, low], axis=0)

    def tmpl_z(self):
        angle = phases(np.arange(TEMPL) - HALF, np.arange(self.kz), self.lz)
        cos = np.zeros((ZF, ZF))
        sin = np.zeros((ZF, ZF))
        cos[:TEMPL, : self.kz] = np.cos(angle)
        sin[:TEMPL, : self.kz] = np.sin(angle)
        none = np.zeros_like(cos)
        return np.block([[cos, none, sin, none], [none, cos, none, sin]])

    def inverse_rows(self, points, count, length, k_pad, tail):
        angle = phases(points, np.arange(count), length)
        weight = np.full((1, count), 1.0 / length)
        weight[0, 0] *= 0.5
        weight[0, count - 1] *= 0.5
        cos = padded_cols(np.cos(angle) * weight, k_pad)
        sin = padded_cols(np.sin(angle) * weight, k_pad)
        return padded_cols(np.concatenate([cos, sin], axis=1), tail)

    def inverse_z(self):
        angle = phases(np.arange(self.kz), np.arange(self.zs), self.lz)
        weight = np.full((self.kz, 1), 2.0 / self.lz)
        weight[0] *= 0.5
        weight[self.kz - 1] *= 0.5
        cos = padded_rows(np.cos(angle) * weight, ZF)
        sin = padded_rows(-np.sin(angle) * weight, ZF)
        none = np.zeros_like(cos)
        return np.block([[cos, none], [none, cos], [sin, none], [none, sin]])


def split(value):
    high = value.astype(BF16)
    return high, (value - high.astype(F32)).astype(BF16)


def mm(left, right):
    return jnp.dot(left, right, preferred_element_type=F32)


def rows_product(table, value):
    count = table.shape[0] // 2
    high, low = split(value)
    both = mm(table, high)
    return both[:count] + both[count:] + mm(table[:count], low)


def plus_minus(folded, count, sign):
    cos_re, cos_im = folded[:count, :LANES], folded[:count, LANES:]
    sin_re, sin_im = folded[count:, :LANES], folded[count:, LANES:]
    first = (cos_re - sin_im, cos_im + sin_re)
    second = (cos_re + sin_im, cos_im - sin_re)
    return (first, second) if sign > 0 else (second, first)


def slab_kernel(plan, flags, own, low, high, table_z, table_x, table_y, spectrum, mid):
    kxp, kx = plan.kxp, plan.kx
    rows = 2 * kxp

    def first(j, carry):
        lanes = pl.ds(pl.multiple_of(j * LANES, LANES), LANES)

        def z_stage(ref):
            block = ref[:, lanes]
            return mm(jnp.concatenate([block, block], axis=1), table_z[...])

        low_z = jnp.where(flags[0] > 0, z_stage(low), 0.0)
        high_z = jnp.where(flags[1] > 0, z_stage(high), 0.0)
        strip = jnp.concatenate([low_z, z_stage(own), high_z], axis=0)
        for part in range(2):
            folded = rows_product(table_x[...], strip[:, part * 256 : part * 256 + 256])
            for s, (re, im) in enumerate(plus_minus(folded, kxp, -1)):
                at = pl.ds(pl.multiple_of((2 * j + part) * rows + s * kxp, 8), kxp)
                mid[0, at, :] = re
                mid[1, at, :] = im
        return carry

    lax.fori_loop(0, plan.ys // 2, first, 0)

    def second(k, carry):
        for s in range(2):
            at = pl.ds(k + s * kxp, plan.ys, stride=rows)
            value = jnp.concatenate([mid[0, at, :], mid[1, at, :]], axis=1)
            folded = rows_product(table_y[...], value)
            for u, (re, im) in enumerate(plus_minus(folded, plan.kyp, -1)):
                spectrum[k, s, u, :, :LANES] = re
                spectrum[k, s, u, :, LANES:] = im
        return carry

    lax.fori_loop(0, kx, second, 0)


def slab_spectrum(plan, flags, own, low, high):
    shape = (plan.kx, 2, 2, plan.kyp, 2 * LANES)
    table_z = plan.slab_z()
    table_x = row_tables(plan.folded(plan.kx, plan.kxp, np.arange(plan.lx), plan.lx))
    table_y = row_tables(plan.folded(plan.ky, plan.kyp, np.arange(plan.ys), plan.ly))
    smem = pl.BlockSpec(memory_space=pltpu.SMEM)
    vmem = pl.BlockSpec(memory_space=pltpu.VMEM)
    return pl.pallas_call(
        functools.partial(slab_kernel, plan),
        out_shape=jax.ShapeDtypeStruct(shape, F32),
        in_specs=[smem] + [vmem] * 6,
        out_specs=vmem,
        scratch_shapes=[pltpu.VMEM((2, plan.ys * 2 * plan.kxp, LANES), F32)],
        compiler_params=pltpu.CompilerParams(vmem_limit_bytes=56 << 20),
        name="slab_spectrum",
    )(flags, own, low, high, table_z, table_x, table_y)


def pair_kernel(
    plan, groups, where, bank, mask, spectrum_hbm, table_z, table_x, table_y, table_yi,
    table_xi, table_zi, zsum, ones, *rest
):
    outs, stats, (zed, mid, back, spectrum, sem) = rest[:groups], rest[groups], rest[groups + 1 :]
    kxp, kx, kyp, ys, xs = plan.kxp, plan.kx, plan.kyp, plan.ys, plan.xs
    rows = 2 * kxp
    fetch = pltpu.make_async_copy(spectrum_hbm, spectrum, sem)
    fetch.start()
    chunk = 384
    total = TEMPL * TEMPL
    count = float(TEMPL**3)
    lane = lax.broadcasted_iota(jnp.int32, (1, LANES), 1)
    used = lax.rem(lane, ZF) < TEMPL

    def add_up(i, carry):
        at = pl.ds(pl.multiple_of(i * chunk, chunk), chunk)
        return carry + jnp.sum(bank[at, :].astype(F32).reshape(chunk // 8, 8, LANES), axis=0)

    sums = lax.fori_loop(0, total // chunk, add_up, jnp.zeros((8, LANES), F32))
    mean = jnp.sum(exact(sums, ones[...]), axis=0, keepdims=True) / count

    def add_squares(i, carry):
        at = pl.ds(pl.multiple_of(i * chunk, chunk), chunk)
        off = jnp.where(used, bank[at, :].astype(F32) - mean, 0.0)
        return carry + jnp.sum((off * off).reshape(chunk // 8, 8, LANES), axis=0)

    squares = lax.fori_loop(0, total // chunk, add_squares, jnp.zeros((8, LANES), F32))
    variance = jnp.sum(exact(squares, ones[...]), axis=0, keepdims=True) / count
    factor = 1.0 / (jnp.sqrt(variance + EPSILON) * float(TEMPL) ** 1.5)
    shift = jnp.concatenate([mean, mean], axis=1) * zsum[...]
    scale = jnp.concatenate([factor, factor], axis=1)

    def z_stage(i, carry):
        at = pl.ds(pl.multiple_of(i * chunk, chunk), chunk)
        block = bank[at, :]
        value = mm(jnp.concatenate([block, block], axis=1), table_z[...])
        value = (value - shift) * scale
        zed[0, at, :] = value[:, :LANES]
        zed[1, at, :] = value[:, LANES:]
        return carry

    lax.fori_loop(0, total // chunk, z_stage, 0)

    def x_stage(i, carry):
        at = pl.ds(i, TEMPL, stride=TEMPL)
        value = jnp.concatenate([zed[0, at, :], zed[1, at, :]], axis=1)
        folded = rows_product(table_x[...], value)
        for s, (re, im) in enumerate(plus_minus(folded, kxp, 1)):
            to = pl.ds(pl.multiple_of(i * rows + s * kxp, 8), kxp)
            mid[0, to, :] = re
            mid[1, to, :] = im
        return carry

    lax.fori_loop(0, TEMPL, x_stage, 0)
    for pad in range(2 * kx, plan.kxi):
        back[:, pad * ys : pad * ys + ys, :] = jnp.zeros((2, ys, LANES), F32)
    fetch.wait()

    def y_stage(k, carry):
        found = []
        for s in range(2):
            at = pl.ds(k + s * kxp, TEMPL, stride=rows)
            value = jnp.concatenate([mid[0, at, :], mid[1, at, :]], axis=1)
            folded = rows_product(table_y[...], value)
            sides = []
            for u, (re, im) in enumerate(plus_minus(folded, kyp, 1)):
                slab_re = spectrum[k, s, u, :, :LANES]
                slab_im = spectrum[k, s, u, :, LANES:]
                sides.append((re * slab_re - im * slab_im, re * slab_im + im * slab_re))
            (re_p, im_p), (re_m, im_m) = sides
            even = jnp.concatenate([re_p + re_m, im_p + im_m], axis=1)
            odd = jnp.concatenate([im_m - im_p, re_p - re_m], axis=1)
            found.append(rows_product(table_yi[...], jnp.concatenate([even, odd], axis=0)))
        even = found[0] + found[1]
        odd = found[0] - found[1]
        to = pl.ds(pl.multiple_of(k * ys, 8), ys)
        back[0, to, :] = even[:, :LANES]
        back[1, to, :] = even[:, LANES:]
        to = pl.ds(pl.multiple_of((k + kx) * ys, 8), ys)
        back[0, to, :] = -odd[:, LANES:]
        back[1, to, :] = odd[:, :LANES]
        return carry

    lax.fori_loop(0, kx, y_stage, 0)
    share = ys // groups
    step = 4
    for j in range(groups):
        base = lax.rem(where[0] + j, groups) * share

        def last(i, carry):
            lines = []
            for part in range(step):
                at = pl.ds(base + i * step + part, plan.kxi, stride=ys)
                value = jnp.concatenate([back[0, at, :], back[1, at, :]], axis=1)
                lines.append(rows_product(table_xi[...], value))
            high, low = split(jnp.concatenate(lines, axis=0))
            both = mm(high, table_zi[...])
            value = both[:, :LANES] + both[:, LANES:] + mm(low, table_zi[:, :LANES])
            outs[j][pl.ds(pl.multiple_of(i * step * xs, 8), step * xs), :] = value
            return carry

        lax.fori_loop(0, share // step, last, 0)
    columns = jnp.sum(mask[...].astype(F32)) * (1.0 / 8.0)
    lane_sum = jnp.zeros((8, LANES), F32)
    for j in range(groups):
        lane_sum += exact(mask[j], outs[j][...])
    lane_mean = lane_sum[:1] / jnp.maximum(columns, 1.0)
    lane_square = jnp.zeros((8, LANES), F32)
    for j in range(groups):
        off = outs[j][...] - lane_mean
        lane_square += exact(mask[j], off * off)
    part_mean = exact(jnp.broadcast_to(lane_mean, (8, LANES)), ones[...]) / float(plan.zs)
    off = lane_mean - part_mean
    part_square = exact(lane_square + columns * off * off, ones[...])
    stats[...] = jnp.concatenate([part_mean[:4], part_square[:4]], axis=0)


def exact(left, right):
    return jnp.dot(left, right, precision=lax.Precision.HIGHEST, preferred_element_type=F32)


def pair_correlation(plan, groups, where, bank, mask, spectrum):
    z_table = plan.tmpl_z()
    ones = np.kron(np.eye(2), np.ones((ZF, ZF))).astype(np.float32)
    tables = [
        row_stack(z_table),
        row_tables(plan.folded(plan.kx, plan.kxp, np.arange(TEMPL), plan.lx)),
        row_tables(plan.folded(plan.ky, plan.kyp, np.arange(TEMPL) - HALF, plan.ly)),
        row_tables(plan.inverse_rows(np.arange(plan.ys), plan.ky, plan.ly, plan.kyp, 2 * plan.kyp)),
        row_tables(plan.inverse_rows(np.arange(plan.xs), plan.kx, plan.lx, plan.kx, plan.kxi)),
        col_tables(plan.inverse_z()),
        z_table.sum(axis=0, keepdims=True).astype(np.float32),
        ones,
    ]
    smem = pl.BlockSpec(memory_space=pltpu.SMEM)
    vmem = pl.BlockSpec(memory_space=pltpu.VMEM)
    share = plan.ys // groups * plan.xs
    return pl.pallas_call(
        functools.partial(pair_kernel, plan, groups),
        out_shape=[jax.ShapeDtypeStruct((share, LANES), F32)] * groups
        + [jax.ShapeDtypeStruct((8, LANES), F32)],
        in_specs=[smem, vmem, vmem, pl.BlockSpec(memory_space=pl.ANY)] + [vmem] * 8,
        out_specs=[vmem] * (groups + 1),
        scratch_shapes=[
            pltpu.VMEM((2, TEMPL * TEMPL, LANES), F32),
            pltpu.VMEM((2, TEMPL * 2 * plan.kxp, LANES), F32),
            pltpu.VMEM((2, plan.kxi * plan.ys, LANES), F32),
            pltpu.VMEM((plan.kx, 2, 2, plan.kyp, 2 * LANES), F32),
            pltpu.SemaphoreType.DMA,
        ],
        compiler_params=pltpu.CompilerParams(vmem_limit_bytes=60 << 20),
        name="pair_correlation",
    )(where, bank, mask, spectrum, *tables)


def row_stack(table):
    return np.concatenate(halves(table), axis=0)


MESH = pl.DeviceIdType.MESH
CORES = 2
RING_X = 4


def place():
    tile = lax.axis_index("tile")
    core = lax.rem(tile, CORES)
    x = lax.rem(tile // CORES, RING_X)
    z = tile // (CORES * RING_X)
    return z, x, core


def tile_of(z, x, core):
    return (z * RING_X + x) * CORES + core


def greet(peers):
    barrier = pltpu.get_barrier_semaphore()
    for peer in peers:
        pl.semaphore_signal(barrier, inc=1, device_id=peer, device_id_type=MESH)
    pl.semaphore_wait(barrier, len(peers))


def stage(source, target, sends, receives, first, peers):
    copies = []
    for index, peer in enumerate(peers):
        copy = pltpu.make_async_remote_copy(
            src_ref=source,
            dst_ref=target,
            send_sem=sends.at[first + index],
            recv_sem=receives.at[first + index],
            device_id=peer,
            device_id_type=MESH,
        )
        copy.start()
        copies.append(copy)
    for copy in copies:
        copy.wait()


def gather_kernel(ring_z, block, out, sends, receives, own_sem):
    z, x, core = place()
    z_peers = [{"tile": tile_of(lax.rem(z + d, ring_z), x, core)} for d in range(1, ring_z)]
    x_peers = [{"tile": tile_of(z, lax.rem(x + d, RING_X), core)} for d in range(1, RING_X)]
    other = [{"tile": tile_of(z, x, 1 - core)}]
    own = pltpu.make_async_copy(block, out.at[core, x, z], own_sem)
    own.start()
    greet(z_peers + x_peers + other)
    own.wait()
    mine = out.at[core, x, z]
    stage(mine, mine, sends, receives, 0, z_peers)
    mine = out.at[core, x]
    stage(mine, mine, sends, receives, len(z_peers), x_peers)
    mine = out.at[core]
    stage(mine, mine, sends, receives, len(z_peers) + len(x_peers), other)


def gathered(block, tiles):
    ring_z = tiles // (CORES * RING_X)
    peers = ring_z + RING_X - 1
    return pl.pallas_call(
        functools.partial(gather_kernel, ring_z),
        out_shape=jax.ShapeDtypeStruct((CORES, RING_X, ring_z) + block.shape, block.dtype),
        in_specs=[pl.BlockSpec(memory_space=pltpu.VMEM)],
        out_specs=pl.BlockSpec(memory_space=pltpu.VMEM),
        scratch_shapes=[
            pltpu.SemaphoreType.DMA((peers,)),
            pltpu.SemaphoreType.DMA((peers,)),
            pltpu.SemaphoreType.DMA,
        ],
        compiler_params=pltpu.CompilerParams(
            collective_id=0, has_side_effects=True, vmem_limit_bytes=32 << 20
        ),
        name="gather_templates",
    )(block)


def stats_kernel(ring_z, groups, first, second, extra, out, sends, receives):
    z, x, core = place()
    rot = lax.axis_index("rot")
    z_peers = [{"tile": tile_of(lax.rem(z + d, ring_z), x, core)} for d in range(1, ring_z)]
    flat = x * CORES + core
    plane = []
    for d in range(1, RING_X * CORES):
        there = lax.rem(flat + d, RING_X * CORES)
        plane.append({"tile": tile_of(z, there // CORES, lax.rem(there, CORES))})
    others = [{"rot": lax.rem(rot + d, groups)} for d in range(1, groups)]
    field = lax.rem(lax.broadcasted_iota(jnp.int32, (1, LANES), 1), ZF)
    row = extra[...]
    for index, value in enumerate((first[0:1], first[4:5], second[0:1], second[4:5])):
        row = jnp.where(field == index, value, row)
    out[rot, flat, z] = row
    greet(z_peers + plane + others)
    mine = out.at[rot, flat, z]
    stage(mine, mine, sends, receives, 0, z_peers)
    mine = out.at[rot, flat]
    stage(mine, mine, sends, receives, len(z_peers), plane)
    mine = out.at[rot]
    stage(mine, mine, sends, receives, len(z_peers) + len(plane), others)


def exchanged(first, second, extra, tiles, groups):
    ring_z = tiles // (CORES * RING_X)
    peers = ring_z + RING_X * CORES + groups - 3
    vmem = pl.BlockSpec(memory_space=pltpu.VMEM)
    return pl.pallas_call(
        functools.partial(stats_kernel, ring_z, groups),
        out_shape=jax.ShapeDtypeStruct((groups, RING_X * CORES, ring_z, 1, LANES), F32),
        in_specs=[vmem] * 3,
        out_specs=vmem,
        scratch_shapes=[pltpu.SemaphoreType.DMA((peers,)), pltpu.SemaphoreType.DMA((peers,))],
        compiler_params=pltpu.CompilerParams(
            collective_id=1, has_side_effects=True, vmem_limit_bytes=32 << 20
        ),
        name="exchange_statistics",
    )(first, second, extra)


FIELD_COUNT = 4
FIELD_QUAT = 5


def final_kernel(groups, xs, zs, where, valid, stats, *rest):
    parts = [rest[2 * j : 2 * j + 2] for j in range(groups)]
    best, evidence, moments = rest[2 * groups : 2 * groups + 3]
    lane = lax.broadcasted_iota(jnp.int32, (1, LANES), 1)
    low_half = lane < ZF

    def spread_field(rows, index):
        return jnp.where(low_half, rows[:, index : index + 1], rows[:, ZF + index : ZF + index + 1])

    terms = []
    for j in range(groups):
        group = lax.rem(where[0] + groups - j, groups)
        rows = stats[group]
        rows = rows.reshape(-1, LANES)
        columns = spread_field(rows, FIELD_COUNT)
        total = jnp.sum(columns, axis=0, keepdims=True)
        for p in range(2):
            mean = spread_field(rows, 2 * p)
            square = spread_field(rows, 2 * p + 1)
            average = jnp.sum(columns * mean, axis=0, keepdims=True) / total
            off = mean - average
            square = jnp.sum(square + (zs * columns) * off * off, axis=0, keepdims=True)
            inverse = 1.0 / jnp.sqrt(square / (total * zs) + EPSILON)
            quat = [spread_field(rows[:1], FIELD_QUAT + 4 * p + c) for c in range(4)]
            terms.append((parts[j][p], average, inverse, quat))

    def column(y):
        at = pl.ds(pl.multiple_of(y * xs, 8), xs)
        scores = [(ref[at, :] - average) * inverse for ref, average, inverse, _ in terms]
        high = functools.reduce(jnp.maximum, scores)
        high = jnp.maximum(high, pltpu.roll(high, ZF, 1))
        weights = [jnp.exp(score - high) for score in scores]
        sums = [functools.reduce(jnp.add, weights)]
        for c in range(4):
            sums.append(functools.reduce(jnp.add, [w * t[3][c] for w, t in zip(weights, terms)]))
        return [high] + [value + pltpu.roll(value, ZF, 1) for value in sums]

    for j in range(valid.shape[1] // 2):
        both = [jnp.where(low_half, a, b) for a, b in zip(column(2 * j), column(2 * j + 1))]
        inside = jnp.where(low_half, valid[:, 2 * j : 2 * j + 1], valid[:, 2 * j + 1 : 2 * j + 2])
        inside = inside.astype(F32)
        high, total = both[0], both[1]
        lanes = slice(j * LANES, j * LANES + LANES)
        best[:, lanes] = inside * high
        evidence[:, lanes] = inside * (high + jnp.log(total))
        ratio = inside / total
        for c in range(4):
            moments[c, :, lanes] = both[2 + c] * ratio


def finished(where, valid, stats, parts, zs):
    groups = len(parts)
    xs, share = valid.shape
    smem = pl.BlockSpec(memory_space=pltpu.SMEM)
    vmem = pl.BlockSpec(memory_space=pltpu.VMEM)
    flat = jax.ShapeDtypeStruct((xs, share * zs), F32)
    return pl.pallas_call(
        functools.partial(final_kernel, groups, xs, zs),
        out_shape=[flat, flat, jax.ShapeDtypeStruct((4, xs, share * zs), F32)],
        in_specs=[smem] + [vmem] * (2 + 2 * groups),
        out_specs=[vmem] * 3,
        compiler_params=pltpu.CompilerParams(vmem_limit_bytes=48 << 20),
        name="finish",
    )(where, valid, stats, *[ref for part in parts for ref in part])


def local(tomogram, templates, valid, quats, rot_index):
    xs, voxels = tomogram.shape
    ys = valid.shape[1]
    zs = voxels // ys
    plan = Plan(xs, ys, zs)
    tiles, groups = lax.axis_size("tile"), lax.axis_size("rot")
    tile, rot = lax.axis_index("tile"), lax.axis_index("rot")
    share = ys // groups
    where = rot.astype(jnp.int32).reshape(1)
    forward = [(i, i + 1) for i in range(tiles - 1)]
    backward = [(i + 1, i) for i in range(tiles - 1)]
    low = lax.ppermute(tomogram[xs - HALF :], "tile", forward)
    high = lax.ppermute(tomogram[:HALF], "tile", backward)
    flags = jnp.stack([tile > 0, tile < tiles - 1]).astype(jnp.int32)
    bank = gathered(templates, tiles)
    per = templates.shape[1] // TEMPL
    bank = bank.reshape(CORES, RING_X, -1, 2, 2, per, TEMPL).transpose(3, 2, 1, 0, 5, 4, 6)
    bank = jnp.pad(bank, [(0, 0)] * 6 + [(0, ZF - TEMPL)]).reshape(2, TEMPL * TEMPL, LANES)
    spectrum = slab_spectrum(plan, flags, tomogram, low, high)
    turned = jnp.roll(valid.T.reshape(groups, share * xs), -rot, axis=0)
    mask = jnp.broadcast_to(turned.astype(F32)[:, None, :], (groups, 8, share * xs))
    columns = jnp.sum(valid).astype(F32)
    one_hot = rot_index[:, None] == jnp.arange(quats.shape[1], dtype=jnp.int32)[None, :]
    orient = jnp.sum(jnp.where(one_hot[:, None, :], quats[None], 0.0), axis=2)
    fields = orient.reshape(2, 2, 4).transpose(1, 0, 2).reshape(2, 8)
    extra = jnp.concatenate(
        [jnp.zeros((2, 4), F32), jnp.full((2, 1), columns), fields, jnp.zeros((2, ZF - 13), F32)],
        axis=1,
    ).reshape(1, LANES)
    received, stats = [], []
    for p in range(2):
        *chunks, stat = pair_correlation(plan, groups, where, bank[p], mask, spectrum)
        stats.append(stat)
        received.append(
            [chunks[0]]
            + [
                lax.ppermute(chunks[j], "rot", [(i, (i + j) % groups) for i in range(groups)])
                for j in range(1, groups)
            ]
        )
    rows = exchanged(stats[0], stats[1], extra, tiles, groups).reshape(groups, tiles, 1, LANES)
    own_valid = lax.dynamic_slice_in_dim(valid, rot * share, share, 1)
    parts = [[received[0][j], received[1][j]] for j in range(groups)]
    return tuple(finished(where, own_valid, rows, parts, zs))


def solution(mesh):
    placed = (P("tile", None), P("rot", "tile"), P("tile", None), P(), P("rot"))
    return jax.shard_map(
        local,
        mesh=mesh,
        in_specs=placed,
        out_specs=(P("tile", "rot"), P("tile", "rot"), P(None, "tile", "rot")),
        check_vma=False,
    )
```

time: 690 us -> 234 us (0.34)
  blocking collectives: 307 us -> 0 us
  Pallas kernels: 0 us -> 198 us
  waiting for transfers between devices: 127 us -> 0.02 us
  matrix products: 101 us -> 0 us
  other arithmetic: 56.8 us -> 1.69 us
  local copies, waits for them, and re-layouts: 68.8 us -> 16.6 us
  between operations: 15.1 us -> 1.49 us
  starting transfers between devices: 6.52 us -> 15.2 us
    psum x2 -> x0, blocking collectives: 251 us -> none  [the longest x1 127 us: local(): lax.psum(jnp.sum(inside[None] * deviation * deviation, axis=(1, 2)), 'tile')]
    pallas_call x0 -> x6, Pallas kernels: none -> 198 us  [the longest x2 109 us: pair_correlation(): pl.pallas_call(functools.partial(pair_kernel, plan, groups), out_shape=[j...]
    dot_general x29 -> x0, matrix products: 101 us -> none  [product(): jnp.einsum(formula, left_arr, right_arr, precision=lax.Precision.HIGH, pr...]
    psum x1 -> x0, waiting for transfers between devices: 85.2 us -> none  [local(): lax.psum((exp_total * rescale, moment * rescale[None]), 'rot')]
    all_gather x1 -> x0, blocking collectives: 55.7 us -> none  [local(): lax.all_gather(templates, 'tile', axis=1, tiled=True).astype(jnp.float32)]
    pmax x1 -> x0, waiting for transfers between devices: 41.4 us -> none  [local(): high_full = lax.pmax(highest, 'rot')]
    transpose x5 -> x2, local copies, waits for them, and re-layouts: 27.7 us -> 0.09 us  [the longest x1 0.08 us: local(): turned = jnp.roll(valid.T.reshape(groups, share * xs), -rot, axis=0)]
    sub x4 -> x0, other arithmetic: 23.7 us -> none  [multiply(): first_arr[0] * other_arr[0] - first_arr[1] * other_arr[1]]
  transfers between devices with their start and end apart: 4 -> 8, of which waited for: 2 -> 0; matrix products, arithmetic and copies ran while one was open for 2% -> 6% of each run, Pallas kernels for 0% -> 43%
where the time goes in v1:
time: 234 us; the launch traced here: 233 us
  Pallas kernels  198 us (85%)
  local copies, waits for them, and re-layouts  16.6 us (7%)
  starting transfers between devices  15.2 us (6%)
    pallas_call x2, Pallas kernels, pair_correlation(): pl.pallas_call(functools.partial(pair_kernel, plan, groups), out_shape=[j...  109 us
    pallas_call x1, Pallas kernels, slab_spectrum(): pl.pallas_call(functools.partial(slab_kernel, plan), out_shape=jax.ShapeD...  35.8 us
    pallas_call x1, Pallas kernels, exchanged(): pl.pallas_call(functools.partial(stats_kernel, ring_z, groups), out_shape...  24.7 us
    pallas_call x1, Pallas kernels, gathered(): pl.pallas_call(functools.partial(gather_kernel, ring_z), out_shape=jax.Sh...  22.2 us
    ppermute x6, starting transfers between devices, local(): lax.ppermute(chunks[j], 'rot', [(i, (i + j) % groups) for i in range(grou...  8.11 us
    pallas_call x1, Pallas kernels, finished(): pl.pallas_call(functools.partial(final_kernel, groups, xs, zs), out_shape...  6.44 us
    slice x3, local copies, waits for them, and re-layouts, local(): bank[p]  6.12 us
    ppermute x1, starting transfers between devices, local(): high = lax.ppermute(tomogram[:HALF], 'tile', backward)  5.14 us
  transfers between devices with their start and end apart: 8, of which 0 were waited for; matrix products, arithmetic and copies ran while one was open for 6% of the time, Pallas kernels for 43%

profile of v1, /device:TPU:1, one launch (start us, length us, event | category | flops | bytes accessed | tf_op | source)
XLA Modules:
  0.0 233.3 jit_solution(3227797141476638661)
XLA Ops:
  0.6 1.9 fusion.2
  2.5 5.1 %collective-permute-start.1 = (bf16[24,5120]{1,0:T(8,128)(2,1)}, bf16[24,5120]{1,0:T(8,128)(2,1)}, u32[]{:S(2)}, u32[]{:S(2)}) collective-permute-start(bf16[24,5120]{1,0:T(8,128)(2,1)} %get-tuple-element.25), channel_id=1, source_target_pairs={{4,0},{8,4},{12,8},{16,12},{20,16},{24,20},{28,24},{32,28},{36,32}... | collective-permute-start | bytes 737288 | tf_op jit(solution)/shard_map/ppermute | solution.py:547
  7.7 1.9 collective-permute-start
  9.6 0.0 copy-start.2
  9.6 0.7 copy-done.2
  10.3 22.2 %gather_templates.1 = bf16[2,4,8,4,1728]{4,3,2,1,0:T(4,128)(2,1)S(1)} custom-call(bf16[4,1728]{1,0:T(4,128)(2,1)S(1)} %copy-done.2), custom_call_target="tpu_custom_call" | custom-call | tf_op jit(solution)/shard_map/gather_templates/pallas_call | solution.py:407
  32.5 0.1 copy.34
  32.6 2.2 reshape.52
  34.8 0.0 copy-start.6
  34.8 2.4 %pad_slice_fusion = (bf16[1,8,4,2,36,2,64]{6,4,1,5,0,2,3:T(8,128)(2,1)}, bf16[1,8,4,2,36,2,64]{6,4,1,5,0,2,3:T(8,128)(2,1)}) fusion(bf16[2,8,4,2,36,2,48]{6,4,1,5,0,2,3:T(8,128)(2,1)S(1)} %bitcast.15), kind=kLoop, calls=%fused_computation | loop fusion | bytes 2064384 | tf_op jit(solution)/shard_map/slice | solution.py:566
  37.2 0.0 copy-done.6
  37.2 0.1 copy.36
  37.3 0.1 reshape.53
  37.4 2.5 %copy.37 = bf16[1,8,4,2,36,2,64]{6,5,4,3,2,1,0:T(2,128)(2,1)S(1)} copy(bf16[1,8,4,2,36,2,64]{6,4,1,5,0,2,3:T(8,128)(2,1)} %get-tuple-element.23) | data formatting | bytes 1179648 | tf_op jit(solution)/shard_map/slice | solution.py:566
  39.9 1.4 squeeze.7.bank
  41.3 0.6 add_convert_fusion.flags
  41.9 0.0 collective-permute-done.1.high
  41.9 0.0 collective-permute-done.low
  41.9 35.8 %slab_spectrum.1.spectrum_hbm = f32[41,2,2,56,256]{4,3,2,1,0:T(8,128)} custom-call(s32[2]{0:T(128)} %add_convert_fusion.flags, bf16[32,5120]{1,0:T(8,128)(2,1)} %own.1, bf16[24,5120]{1,0:T(8,128)(2,1)} %collective-permute-done.low, bf16[24,5120]{1,0:T(8,128)(2,1)} %collective-permute-done.1.high, bf16[256,512]{1,0:T(8,128)(2,1)} %constant.66.clone.table_z, ...), custom_call_target="tpu_custom_call" | custom-call | tf_op jit(solution)/shard_map/slab_spectrum/pallas_call | solution.py:175
  77.7 0.6 broadcast_in_dim.36.mask
  78.4 0.0 copy-start.8
  78.4 0.0 copy-start.7
  78.4 0.0 copy-start.5
  78.4 54.6 %pair_correlation.3 = (f32[640,128]{1,0:T(8,128)}, f32[640,128]{1,0:T(8,128)}, f32[640,128]{1,0:T(8,128)}, f32[640,128]{1,0:T(8,128)}, f32[8,128]{1,0:T(8,128)}) custom-call(s32[1]{0:T(128)} %bitcast.where, bf16[2304,128]{1,0:T(8,128)(2,1)} %squeeze.7.bank, f32[4,8,640]{2,1,0:T(8,128)} %broadcast_in_dim.36.mask, ...), custom_call_target="tpu_custom_call" | custom-call | tf_op jit(solution)/shard_map/pair_correlation/pallas_call | solution.py:324
  133.0 1.6 collective-permute-start.3
  134.6 0.0 copy-done.8
  134.6 0.1 iota_compare_fusion
  134.7 0.6 reduce_sum.18
  136.0 0.0 copy-done.7
  136.0 0.2 select_reduce_fusion
  136.2 0.1 reshape.55
  136.3 0.0 copy-done.5
  136.3 1.2 copy.35
  137.5 1.4 squeeze.6.bank
  138.9 0.1 pad.8.clone
  138.9 0.1 pad_maximum_fusion
  139.0 0.0 copy-start.10
  139.0 0.0 copy-start.9
  139.0 0.0 copy-start.3
  139.0 0.0 copy-start
  139.0 54.6 %pair_correlation.2 = (f32[640,128]{1,0:T(8,128)}, f32[640,128]{1,0:T(8,128)}, f32[640,128]{1,0:T(8,128)}, f32[640,128]{1,0:T(8,128)}, f32[8,128]{1,0:T(8,128)}) custom-call(s32[1]{0:T(128)} %bitcast.where, bf16[2304,128]{1,0:T(8,128)(2,1)} %squeeze.6.bank, f32[4,8,640]{2,1,0:T(8,128)} %broadcast_in_dim.36.mask, ...), custom_call_target="tpu_custom_call" | custom-call | tf_op jit(solution)/shard_map/pair_correlation/pallas_call | solution.py:324
  193.6 0.0 copy-done.10
  193.7 2.7 %collective-permute-start.5 = (f32[640,128]{1,0:T(8,128)S(1)}, f32[640,128]{1,0:T(8,128)S(1)}, u32[]{:S(2)}, u32[]{:S(2)}) collective-permute-start(f32[640,128]{1,0:T(8,128)S(1)} %copy-done.10), channel_id=1, source_target_pairs={{0,2},{1,3},{2,0},{3,1},{4,6},{5,7},{6,4},{7,5},{8,10},{9,11},{10,... | collective-permute-start | bytes 983048 | tf_op jit(solution)/shard_map/ppermute | solution.py:571
  196.3 0.0 copy-done.9
  196.3 1.1 collective-permute-start.7
  197.4 0.4 collective-permute-start.2
  197.8 0.8 collective-permute-start.4
  198.6 0.0 collective-permute-done.3.rest_3_
  198.6 1.6 collective-permute-start.6
  200.2 0.1 maximum_maximum_fusion
  200.3 0.1 reshape.56.extra
  200.4 0.1 constant_dynamic-slice_fusion.valid
  200.4 0.0 copy-done.3
  200.4 0.7 copy-done.4
  201.1 24.7 %exchange_statistics.1 = f32[4,8,8,1,128]{4,3,2,1,0:T(1,128)S(1)} custom-call(f32[8,128]{1,0:T(8,128)S(1)} %copy-done.4, f32[8,128]{1,0:T(8,128)S(1)} %copy-done.3, f32[1,128]{1,0:T(1,128)S(1)} %reshape.56.extra), custom_call_target="tpu_custom_call" | custom-call | tf_op jit(solution)/shard_map/exchange_statistics/pallas_call | solution.py:452
  225.8 0.0 collective-permute-done.5.rest_5_
  225.8 0.0 collective-permute-done.7.rest_7_
  225.8 0.0 collective-permute-done.2.rest_2_
  225.9 0.0 collective-permute-done.4.rest_4_
  225.9 0.0 collective-permute-done.6.rest_6_
  225.9 0.0 copy-done
  225.9 0.0 copy-start.1
  225.9 1.0 copy-done.1
  226.9 6.4 %finish.1 = (f32[32,1280]{1,0:T(8,128)}, f32[32,1280]{1,0:T(8,128)}, f32[4,32,1280]{2,1,0:T(8,128)}) custom-call(s32[1]{0:T(128)} %bitcast.where, s32[32,20]{1,0:T(8,128)S(1)} %constant_dynamic-slice_fusion.valid, f32[4,64,1,128]{3,2,1,0:T(1,128)S(1)} %bitcast.14, f32[640,128]{1,0:T(8,128)S(1)} %copy-done.1, f32[640,128]{1,0:T(8,128)S(1)} %copy-done, ...), custom_call_target="tpu_custom_call" | custom-call | tf_op jit(solution)/shard_map/finish/pallas_call | solution.py:525
  (5 shorter events, 0.0 us)
Async XLA Ops:
  2.5 39.4 %collective-permute-start.1 = (bf16[24,5120]{1,0:T(8,128)(2,1)}, bf16[24,5120]{1,0:T(8,128)(2,1)}, u32[]{:S(2)}, u32[]{:S(2)}) collective-permute-start(bf16[24,5120]{1,0:T(8,128)(2,1)} %get-tuple-element.25), channel_id=1, source_target_pairs={{4,0},{8,4},{12,8},{16,12},{20,16},{24,20},{28,24},{32,28},{36,32}... | collective-permute-start | bytes 737288 | tf_op jit(solution)/shard_map/ppermute | solution.py:547
  7.7 34.2 %collective-permute-start = (bf16[24,5120]{1,0:T(8,128)(2,1)}, bf16[24,5120]{1,0:T(8,128)(2,1)}, u32[]{:S(2)}, u32[]{:S(2)}) collective-permute-start(bf16[24,5120]{1,0:T(8,128)(2,1)} %get-tuple-element.26), channel_id=1, source_target_pairs={{0,4},{4,8},{8,12},{12,16},{16,20},{20,24},{24,28},{28,32},{32,36}... | collective-permute-start | bytes 737288 | tf_op jit(solution)/shard_map/ppermute | solution.py:546
  9.6 0.7 copy-start.2
  34.8 2.4 %copy-start.6 = (s32[32,80]{1,0:T(8,128)S(1)}, s32[32,80]{1,0:T(8,128)}, u32[]{:S(2)}) copy-start(s32[32,80]{1,0:T(8,128)} %param.26) | copy-start | bytes 30724
  78.4 56.2 %copy-start.8 = (s32[4]{0:T(128)S(1)}, s32[4]{0:T(128)}, u32[]{:S(2)}) copy-start(s32[4]{0:T(128)} %param.28) | copy-start | bytes 52
  78.4 57.6 %copy-start.7 = (f32[4,4096]{1,0:T(4,128)S(1)}, f32[4,4096]{1,0:T(4,128)}, u32[]{:S(2)}) copy-start(f32[4,4096]{1,0:T(4,128)} %param.27) | copy-start | bytes 196612
  78.4 57.9 %copy-start.5 = (bf16[1,8,4,2,36,2,64]{6,4,1,5,0,2,3:T(8,128)(2,1)S(1)}, bf16[1,8,4,2,36,2,64]{6,4,1,5,0,2,3:T(8,128)(2,1)}, u32[]{:S(2)}) copy-start(bf16[1,8,4,2,36,2,64]{6,4,1,5,0,2,3:T(8,128)(2,1)} %get-tuple-element.24) | copy-start | bytes 1769476
  133.0 65.6 %collective-permute-start.3 = (f32[640,128]{1,0:T(8,128)}, f32[640,128]{1,0:T(8,128)S(1)}, u32[]{:S(2)}, u32[]{:S(2)}) collective-permute-start(f32[640,128]{1,0:T(8,128)} %get-tuple-element.18), channel_id=1, source_target_pairs={{0,1},{1,2},{2,3},{3,0},{4,5},{5,6},{6,7},{7,4},{8,9},{9,10},{10,1... | collective-permute-start | bytes 983048 | tf_op jit(solution)/shard_map/ppermute | solution.py:571
  139.0 54.6 %copy-start.10 = (f32[640,128]{1,0:T(8,128)S(1)}, f32[640,128]{1,0:T(8,128)}, u32[]{:S(2)}) copy-start(f32[640,128]{1,0:T(8,128)} %get-tuple-element.20) | copy-start | bytes 983044
  139.0 57.3 %copy-start.9 = (f32[640,128]{1,0:T(8,128)S(1)}, f32[640,128]{1,0:T(8,128)}, u32[]{:S(2)}) copy-start(f32[640,128]{1,0:T(8,128)} %get-tuple-element.22) | copy-start | bytes 983044
  139.0 61.4 %copy-start.3 = (f32[8,128]{1,0:T(8,128)S(1)}, f32[8,128]{1,0:T(8,128)}, u32[]{:S(2)}) copy-start(f32[8,128]{1,0:T(8,128)} %get-tuple-element.14.second) | copy-start | bytes 12292
  139.0 86.8 %copy-start = (f32[640,128]{1,0:T(8,128)S(1)}, f32[640,128]{1,0:T(8,128)}, u32[]{:S(2)}) copy-start(f32[640,128]{1,0:T(8,128)} %get-tuple-element.16.rest_1_) | copy-start | bytes 983044
  193.7 32.2 %collective-permute-start.5 = (f32[640,128]{1,0:T(8,128)S(1)}, f32[640,128]{1,0:T(8,128)S(1)}, u32[]{:S(2)}, u32[]{:S(2)}) collective-permute-start(f32[640,128]{1,0:T(8,128)S(1)} %copy-done.10), channel_id=1, source_target_pairs={{0,2},{1,3},{2,0},{3,1},{4,6},{5,7},{6,4},{7,5},{8,10},{9,11},{10,... | collective-permute-start | bytes 983048 | tf_op jit(solution)/shard_map/ppermute | solution.py:571
  196.3 29.5 %collective-permute-start.7 = (f32[640,128]{1,0:T(8,128)S(1)}, f32[640,128]{1,0:T(8,128)S(1)}, u32[]{:S(2)}, u32[]{:S(2)}) collective-permute-start(f32[640,128]{1,0:T(8,128)S(1)} %copy-done.9), channel_id=1, source_target_pairs={{0,3},{1,0},{2,1},{3,2},{4,7},{5,4},{6,5},{7,6},{8,11},{9,8},{10,9... | collective-permute-start | bytes 983048 | tf_op jit(solution)/shard_map/ppermute | solution.py:571
  197.4 28.4 %collective-permute-start.2 = (f32[640,128]{1,0:T(8,128)}, f32[640,128]{1,0:T(8,128)S(1)}, u32[]{:S(2)}, u32[]{:S(2)}) collective-permute-start(f32[640,128]{1,0:T(8,128)} %get-tuple-element.17), channel_id=1, source_target_pairs={{0,1},{1,2},{2,3},{3,0},{4,5},{5,6},{6,7},{7,4},{8,9},{9,10},{10,1... | collective-permute-start | bytes 983048 | tf_op jit(solution)/shard_map/ppermute | solution.py:571
  197.8 28.0 %collective-permute-start.4 = (f32[640,128]{1,0:T(8,128)}, f32[640,128]{1,0:T(8,128)S(1)}, u32[]{:S(2)}, u32[]{:S(2)}) collective-permute-start(f32[640,128]{1,0:T(8,128)} %get-tuple-element.19), channel_id=1, source_target_pairs={{0,2},{1,3},{2,0},{3,1},{4,6},{5,7},{6,4},{7,5},{8,10},{9,11},{10,... | collective-permute-start | bytes 983048 | tf_op jit(solution)/shard_map/ppermute | solution.py:571
  198.6 27.3 %collective-permute-start.6 = (f32[640,128]{1,0:T(8,128)}, f32[640,128]{1,0:T(8,128)S(1)}, u32[]{:S(2)}, u32[]{:S(2)}) collective-permute-start(f32[640,128]{1,0:T(8,128)} %get-tuple-element.21), channel_id=1, source_target_pairs={{0,3},{1,0},{2,1},{3,2},{4,7},{5,4},{6,5},{7,6},{8,11},{9,8},{10,9... | collective-permute-start | bytes 983048 | tf_op jit(solution)/shard_map/ppermute | solution.py:571
  200.4 0.7 copy-start.4
  225.9 1.0 copy-start.1

commit v2 on v0

v2 whole, which is shorter than its diff:
```python
import functools
import math

import jax
import jax.numpy as jnp
import ml_dtypes
import numpy as np
from jax import lax
from jax.experimental import pallas as pl
from jax.experimental.pallas import tpu as pltpu
from jax.sharding import PartitionSpec as P

TEMPL = 48
HALF = 24
EPSILON = 1e-06
LANES = 128
ZF = 64
CORES = 2
RING_X = 4
BLOCK = 48
MESH = pl.DeviceIdType.MESH
FIELD_COUNT = 4
FIELD_QUAT = 5
F32 = jnp.float32
BF16 = jnp.bfloat16


def halves(table):
    high = table.astype(np.float32).astype(ml_dtypes.bfloat16)
    low = (table - high.astype(np.float64)).astype(np.float32).astype(ml_dtypes.bfloat16)
    return high, low


def row_tables(table):
    high, low = halves(table)
    return np.concatenate([high, low], axis=0)


def col_tables(table):
    high, low = halves(table)
    return np.concatenate([high, low], axis=1)


def phases(rows, cols, length):
    index = np.outer(np.asarray(rows), np.asarray(cols)) % length
    return index * (2.0 * np.pi / length)


def padded_rows(table, rows):
    return np.pad(table, ((0, rows - table.shape[0]), (0, 0)))


def padded_cols(table, cols):
    return np.pad(table, ((0, 0), (0, cols - table.shape[1])))


def up8(n):
    return -(-n // 8) * 8


class Plan:
    def __init__(self, xs, ys, zs):
        self.xs, self.ys, self.zs = xs, ys, zs
        self.lx, self.ly, self.lz = xs + TEMPL, ys + HALF, zs + HALF
        self.kx, self.ky, self.kz = self.lx // 2 + 1, self.ly // 2 + 1, self.lz // 2 + 1
        self.kxp, self.kyp = up8(self.kx), up8(self.ky)
        self.kxc = -(-self.kx // 4) * 4
        self.kxi = 2 * self.kxc

    def folded(self, count, pad, points, length):
        angle = phases(np.arange(count), points, length)
        return np.concatenate(
            [padded_rows(np.cos(angle), pad), padded_rows(np.sin(angle), pad)], axis=0
        )

    def slab_z(self):
        angle = phases(np.arange(self.zs), np.arange(self.kz), self.lz)
        cos = padded_cols(np.cos(angle), ZF)
        sin = padded_cols(-np.sin(angle), ZF)
        one = np.concatenate([cos, cos, sin, sin], axis=1)
        none = np.zeros_like(one)
        high, low = halves(np.block([[one, none], [none, one]]))
        return np.concatenate([high, low], axis=0)

    def tmpl_z(self):
        angle = phases(np.arange(TEMPL) - HALF, np.arange(self.kz), self.lz)
        cos = np.zeros((ZF, ZF))
        sin = np.zeros((ZF, ZF))
        cos[:TEMPL, : self.kz] = np.cos(angle)
        sin[:TEMPL, : self.kz] = np.sin(angle)
        none = np.zeros_like(cos)
        return np.block([[cos, none, sin, none], [none, cos, none, sin]])

    def inverse_rows(self, points, count, length, k_pad, tail):
        angle = phases(points, np.arange(count), length)
        weight = np.full((1, count), 1.0 / length)
        weight[0, 0] *= 0.5
        weight[0, count - 1] *= 0.5
        cos = padded_cols(np.cos(angle) * weight, k_pad)
        sin = padded_cols(np.sin(angle) * weight, k_pad)
        return padded_cols(np.concatenate([cos, sin], axis=1), tail)

    def inverse_z(self):
        angle = phases(np.arange(self.kz), np.arange(self.zs), self.lz)
        weight = np.full((self.kz, 1), 2.0 / self.lz)
        weight[0] *= 0.5
        weight[self.kz - 1] *= 0.5
        cos = padded_rows(np.cos(angle) * weight, ZF)
        sin = padded_rows(-np.sin(angle) * weight, ZF)
        none = np.zeros_like(cos)
        return np.block([[cos, none], [none, cos], [sin, none], [none, sin]])


def unrolled(body, count):
    def many(i, carry):
        return lax.fori_loop(0, count, lambda part, c: body(i * count + part, c), carry, unroll=True)

    return many


def split(value):
    high = value.astype(BF16)
    return high, (value - high.astype(F32)).astype(BF16)


def mm(left, right):
    return jnp.dot(left, right, preferred_element_type=F32)


def rows_product(table, value):
    count = table.shape[0] // 2
    high, low = split(value)
    both = mm(table, high)
    return both[:count] + both[count:] + mm(table[:count], low)


def stacked_table(table):
    high, low = halves(table)
    return np.concatenate([high, high, low], axis=1)


def stacked_product(table, value):
    high, low = split(value)
    return mm(table, jnp.concatenate([high, low, high], axis=0))


def paired_table(table):
    high, low = halves(table)
    return np.block([[high, high], [low, np.zeros_like(low)]])


def paired_product(table, value):
    high, low = split(value)
    count = table.shape[0] // 2
    both = mm(table, jnp.concatenate([high, low], axis=0))
    return both[:count] + both[count:]


def plus_minus(folded, count, sign):
    cos_re, cos_im = folded[:count, :LANES], folded[:count, LANES:]
    sin_re, sin_im = folded[count:, :LANES], folded[count:, LANES:]
    first = (cos_re - sin_im, cos_im + sin_re)
    second = (cos_re + sin_im, cos_im - sin_re)
    return (first, second) if sign > 0 else (second, first)


def exact(left, right):
    return jnp.dot(left, right, precision=lax.Precision.HIGHEST, preferred_element_type=F32)


def tall_sum(value):
    return jnp.sum(value.reshape(-1, 8, value.shape[-1]), axis=0)


def tile_of(z, x, core):
    return (z * RING_X + x) * CORES + core


def greet(peers):
    barrier = pltpu.get_barrier_semaphore()
    for peer in peers:
        pl.semaphore_signal(barrier, inc=1, device_id=peer, device_id_type=MESH)
    pl.semaphore_wait(barrier, len(peers))


def remote(source, target, sends, receives, index, peer):
    return pltpu.make_async_remote_copy(
        src_ref=source,
        dst_ref=target,
        send_sem=sends.at[index],
        recv_sem=receives.at[index],
        device_id=peer,
        device_id_type=MESH,
    )


def begin(source, target, sends, receives, first, peers):
    copies = [
        remote(source, target, sends, receives, first + index, peer)
        for index, peer in enumerate(peers)
    ]
    for copy in copies:
        copy.start()
    return copies


def finish(copies):
    for copy in copies:
        copy.wait()


def match_kernel(
    plan, tiles, groups, own, block, valid, extra, slab_z, slab_x, slab_y, table_z, table_x,
    table_y, table_yi, table_xi, table_zi, zsum, ones, parts, stats, low, high, bank, spectrum,
    slab_mid, zed, mid, back, marks, ready, row, sends, receives, part_sends, part_receives,
):
    ring_z = tiles // (CORES * RING_X)
    plane_size = RING_X * CORES
    kxp, kyp, ys, xs = plan.kxp, plan.kyp, plan.ys, plan.xs
    rows = 2 * kxp
    tile, rot = lax.axis_index("tile"), lax.axis_index("rot")
    core = lax.rem(tile, CORES)
    x = lax.rem(tile // CORES, RING_X)
    z = tile // (CORES * RING_X)
    flat = x * CORES + core
    z_peers = [{"tile": tile_of(lax.rem(z + d, ring_z), x, core)} for d in range(1, ring_z)]
    x_peers = [{"tile": tile_of(z, lax.rem(x + d, RING_X), core)} for d in range(1, RING_X)]
    other = [{"tile": tile_of(z, x, 1 - core)}]
    plane = []
    for d in range(1, plane_size):
        there = lax.rem(flat + d, plane_size)
        plane.append({"tile": tile_of(z, there // CORES, lax.rem(there, CORES))})
    rot_peers = [{"rot": lax.rem(rot + d, groups)} for d in range(1, groups)]
    after = {"tile": lax.rem(tile + 1, tiles)}
    before = {"tile": lax.rem(tile + tiles - 1, tiles)}

    bank[core, x, z] = block[...]
    greet([after, before] + z_peers + plane + rot_peers)
    halo = [
        remote(own, low, sends, receives, 0, after),
        remote(own, high, sends, receives, 1, before),
    ]
    for copy in halo:
        copy.start()
    mine = bank.at[core, x, z]
    copies = begin(mine, mine, sends, receives, 2, z_peers)

    flags = valid[...].astype(F32)
    columns = jnp.sum(flags)
    for y in range(ys):
        marks[y * xs : y * xs + xs, :] = jnp.broadcast_to(flags[:, y : y + 1], (xs, LANES))
    row[...] = extra[...]
    finish(halo)

    def slab_first(j, carry):
        lanes = pl.ds(pl.multiple_of(j * LANES, LANES), LANES)
        strips = [
            jnp.where(tile > 0, low[:, lanes].astype(F32)[xs - HALF :], 0.0),
            own[:, lanes].astype(F32),
            jnp.where(tile < tiles - 1, high[:, lanes].astype(F32)[:HALF], 0.0),
        ]
        strip = jnp.concatenate(strips, axis=0).astype(BF16)
        strip = mm(jnp.concatenate([strip, strip], axis=1), slab_z[...])
        for part in range(2):
            folded = stacked_product(slab_x[...], strip[:, part * 256 : part * 256 + 256])
            for s, (re, im) in enumerate(plus_minus(folded, kxp, -1)):
                at = pl.ds(pl.multiple_of((2 * j + part) * rows + s * kxp, 8), kxp)
                slab_mid[0, at, :] = re
                slab_mid[1, at, :] = im
        return carry

    trips = ys // 2 // 4
    lax.fori_loop(0, trips // 2, unrolled(slab_first, 4), 0)
    finish(copies)
    mine = bank.at[core, x]
    copies = begin(mine, mine, sends, receives, 1 + ring_z, x_peers)
    lax.fori_loop(trips // 2, trips, unrolled(slab_first, 4), 0)
    finish(copies)
    mine = bank.at[core]
    copies = begin(mine, mine, sends, receives, ring_z + RING_X, other)

    def slab_second(k, carry):
        for s in range(2):
            at = pl.ds(k + s * kxp, ys, stride=rows)
            value = jnp.concatenate([slab_mid[0, at, :], slab_mid[1, at, :]], axis=1)
            folded = stacked_product(slab_y[...], value)
            for u, (re, im) in enumerate(plus_minus(folded, kyp, -1)):
                spectrum[k, s, u, :, :LANES] = re
                spectrum[k, s, u, :, LANES:] = im
        return carry

    lax.fori_loop(0, plan.kxc // 11, unrolled(slab_second, 11), 0)
    finish(copies)

    per = TEMPL * TEMPL // tiles
    total = float(TEMPL**3)
    lane = lax.broadcasted_iota(jnp.int32, (BLOCK, LANES), 1)
    line = lax.broadcasted_iota(jnp.int32, (BLOCK, LANES), 0)
    used = jnp.logical_and(lax.rem(lane, ZF) < TEMPL, line < per)[None]
    field = lax.rem(lax.broadcasted_iota(jnp.int32, (1, LANES), 1), ZF)
    share = ys // groups
    step = share
    tall = ring_z * BLOCK

    def pair(p, outer):
        def add_up(i, carry):
            value = bank[i // RING_X, lax.rem(i, RING_X), :, p].astype(F32)
            return carry + tall_sum(value.reshape(tall, LANES))

        sums = lax.fori_loop(0, plane_size, add_up, jnp.zeros((8, LANES), F32))
        mean = jnp.sum(exact(sums, ones[...]), axis=0, keepdims=True) / total

        def add_squares(i, carry):
            value = bank[i // RING_X, lax.rem(i, RING_X), :, p].astype(F32)
            off = jnp.where(used, value - mean[None], 0.0)
            return carry + tall_sum((off * off).reshape(tall, LANES))

        squares = lax.fori_loop(0, plane_size, add_squares, jnp.zeros((8, LANES), F32))
        variance = jnp.sum(exact(squares, ones[...]), axis=0, keepdims=True) / total
        factor = 1.0 / (jnp.sqrt(variance + EPSILON) * float(TEMPL) ** 1.5)
        shift = jnp.concatenate([mean, mean], axis=1) * zsum[...]
        scale = jnp.concatenate([factor, factor], axis=1)

        def z_stage(i, carry):
            lines = bank[i // RING_X, lax.rem(i, RING_X), :, p].reshape(tall, LANES)
            value = mm(jnp.concatenate([lines, lines], axis=1), table_z[...])
            value = (value - shift) * scale
            at = pl.ds(pl.multiple_of(i * tall, tall), tall)
            zed[0, at, :] = value[:, :LANES]
            zed[1, at, :] = value[:, LANES:]
            return carry

        lax.fori_loop(0, plane_size, z_stage, 0)

        def x_stage(b, carry):
            lines = []
            for s in range(TEMPL // ring_z):
                index = s * TEMPL + b
                owner = index // per
                there = lax.rem(owner, CORES) * RING_X + owner // CORES
                at = pl.ds(there * tall + lax.rem(index, per), ring_z, stride=BLOCK)
                lines.append(jnp.concatenate([zed[0, at, :], zed[1, at, :]], axis=1))
            folded = stacked_product(table_x[...], jnp.concatenate(lines, axis=0))
            for s, (re, im) in enumerate(plus_minus(folded, kxp, 1)):
                to = pl.ds(pl.multiple_of(b * rows + s * kxp, 8), kxp)
                mid[0, to, :] = re
                mid[1, to, :] = im
            return carry

        lax.fori_loop(0, TEMPL // 12, unrolled(x_stage, 12), 0)

        def y_stage(k, carry):
            found = []
            for s in range(2):
                at = pl.ds(k + s * kxp, TEMPL, stride=rows)
                value = jnp.concatenate([mid[0, at, :], mid[1, at, :]], axis=1)
                folded = stacked_product(table_y[...], value)
                sides = []
                for u, (re, im) in enumerate(plus_minus(folded, kyp, 1)):
                    slab_re = spectrum[k, s, u, :, :LANES]
                    slab_im = spectrum[k, s, u, :, LANES:]
                    sides.append((re * slab_re - im * slab_im, re * slab_im + im * slab_re))
                (re_p, im_p), (re_m, im_m) = sides
                even = jnp.concatenate([re_p + re_m, im_p + im_m], axis=1)
                odd = jnp.concatenate([im_m - im_p, re_p - re_m], axis=1)
                found.append(paired_product(table_yi[...], jnp.concatenate([even, odd], axis=0)))
            even = found[0] + found[1]
            odd = found[0] - found[1]
            to = pl.ds(pl.multiple_of(k * ys, 8), ys)
            back[0, to, :] = even[:, :LANES]
            back[1, to, :] = even[:, LANES:]
            to = pl.ds(pl.multiple_of((k + plan.kxc) * ys, 8), ys)
            back[0, to, :] = -odd[:, LANES:]
            back[1, to, :] = odd[:, :LANES]
            return carry

        lax.fori_loop(0, plan.kxc // 11, unrolled(y_stage, 11), 0)

        def last(i, lane_sum):
            j = lax.rem(i + 1, groups)
            base = lax.rem(rot + j, groups) * share
            lines = []
            for y in range(step):
                at = pl.ds(base + y, plan.kxi, stride=ys)
                value = jnp.concatenate([back[0, at, :], back[1, at, :]], axis=1)
                lines.append(rows_product(table_xi[...], value))
            upper, lower = split(jnp.concatenate(lines, axis=0))
            both = mm(upper, table_zi[...])
            value = both[:, :LANES] + both[:, LANES:] + mm(lower, table_zi[:, :LANES])
            ready[p, j] = value

            @pl.when(j > 0)
            def _():
                send_part(p, j).start()

            mark = marks[pl.ds(pl.multiple_of(base * xs, 8), share * xs), :]
            return lane_sum + tall_sum(value * mark)

        def send_part(p, j):
            return pltpu.make_async_remote_copy(
                src_ref=ready.at[p, j],
                dst_ref=parts.at[p, j],
                send_sem=part_sends.at[p, j],
                recv_sem=part_receives.at[p, j],
                device_id={"rot": lax.rem(rot + j, groups)},
                device_id_type=MESH,
            )

        lane_sum = lax.fori_loop(0, groups, last, jnp.zeros((8, LANES), F32))
        parts[p, 0] = ready[p, 0]
        lane_mean = jnp.sum(lane_sum, axis=0, keepdims=True) / jnp.maximum(columns, 1.0)

        def add_off(j, carry):
            base = lax.rem(rot + j, groups) * (share * xs)
            mark = marks[pl.ds(pl.multiple_of(base, 8), share * xs), :]
            off = ready[p, j] - lane_mean
            return carry + tall_sum(off * off * mark)

        lane_square = lax.fori_loop(0, groups, add_off, jnp.zeros((8, LANES), F32))
        wide = jnp.broadcast_to(lane_mean, (8, LANES))
        part_mean = exact(wide, ones[...])[:1] / float(plan.zs)
        off = lane_mean - part_mean
        lane_square = jnp.sum(lane_square, axis=0, keepdims=True) + columns * off * off
        part_square = exact(jnp.broadcast_to(lane_square, (8, LANES)), ones[...])[:1]
        now = jnp.where(field == 2 * p, part_mean, row[...])
        row[...] = jnp.where(field == 2 * p + 1, part_square, now)
        return outer

    lax.fori_loop(0, 2, pair, 0)
    stats[rot, flat, z] = row[...]
    first = 1 + ring_z + RING_X
    mine = stats.at[rot, flat, z]
    finish(begin(mine, mine, sends, receives, first, z_peers))
    mine = stats.at[rot, flat]
    finish(begin(mine, mine, sends, receives, first + ring_z - 1, plane))
    mine = stats.at[rot]
    finish(begin(mine, mine, sends, receives, first + ring_z + plane_size - 2, rot_peers))
    for p in range(2):
        for j in range(1, groups):
            remote(
                ready.at[p, j], parts.at[p, j], part_sends.at[p], part_receives.at[p], j, rot_peers[j - 1]
            ).wait()


def matched(plan, tiles, groups, own, block, valid, extra):
    ring_z = tiles // (CORES * RING_X)
    order = (
        np.arange(TEMPL // ring_z)[:, None] + (TEMPL // ring_z) * np.arange(ring_z)[None]
    ).reshape(-1)
    z_table = plan.tmpl_z()
    tables = [
        plan.slab_z(),
        stacked_table(plan.folded(plan.kx, plan.kxp, np.arange(plan.lx), plan.lx)),
        stacked_table(plan.folded(plan.ky, plan.kyp, np.arange(plan.ys), plan.ly)),
        row_stack(z_table),
        stacked_table(plan.folded(plan.kx, plan.kxp, order, plan.lx)),
        stacked_table(plan.folded(plan.ky, plan.kyp, np.arange(TEMPL) - HALF, plan.ly)),
        paired_table(plan.inverse_rows(np.arange(plan.ys), plan.ky, plan.ly, plan.kyp, 2 * plan.kyp)),
        row_tables(plan.inverse_rows(np.arange(plan.xs), plan.kx, plan.lx, plan.kxc, plan.kxi)),
        col_tables(plan.inverse_z()),
        z_table.sum(axis=0, keepdims=True).astype(np.float32),
        np.kron(np.eye(2), np.ones((ZF, ZF))).astype(np.float32),
    ]
    share = plan.ys // groups * plan.xs
    copies = ring_z + RING_X + 1 + ring_z + RING_X * CORES + groups - 3
    vmem = pl.BlockSpec(memory_space=pltpu.VMEM)
    return pl.pallas_call(
        functools.partial(match_kernel, plan, tiles, groups),
        out_shape=[
            jax.ShapeDtypeStruct((2, groups, share, LANES), F32),
            jax.ShapeDtypeStruct((groups, RING_X * CORES, ring_z, 1, LANES), F32),
        ],
        in_specs=[vmem] * (4 + len(tables)),
        out_specs=[vmem] * 2,
        scratch_shapes=[
            pltpu.VMEM(own.shape, BF16),
            pltpu.VMEM(own.shape, BF16),
            pltpu.VMEM((CORES, RING_X, ring_z) + block.shape, BF16),
            pltpu.VMEM((plan.kxc, 2, 2, plan.kyp, 2 * LANES), F32),
            pltpu.VMEM((2, plan.ys * 2 * plan.kxp, LANES), F32),
            pltpu.VMEM((2, tiles * BLOCK, LANES), F32),
            pltpu.VMEM((2, TEMPL * 2 * plan.kxp, LANES), F32),
            pltpu.VMEM((2, plan.kxi * plan.ys, LANES), F32),
            pltpu.VMEM((plan.ys * plan.xs, LANES), F32),
            pltpu.VMEM((2, groups, share, LANES), F32),
            pltpu.VMEM((1, LANES), F32),
            pltpu.SemaphoreType.DMA((copies,)),
            pltpu.SemaphoreType.DMA((copies,)),
            pltpu.SemaphoreType.DMA((2, groups)),
            pltpu.SemaphoreType.DMA((2, groups)),
        ],
        compiler_params=pltpu.CompilerParams(
            collective_id=0, has_side_effects=True, vmem_limit_bytes=60 << 20
        ),
        name="match",
    )(own, block, valid, extra, *tables)


def row_stack(table):
    return np.concatenate(halves(table), axis=0)


def final_kernel(groups, xs, zs, where, valid, stats, parts, best, evidence, moments):
    lane = lax.broadcasted_iota(jnp.int32, (1, LANES), 1)
    low_half = lane < ZF

    def spread_field(rows, index):
        return jnp.where(low_half, rows[:, index : index + 1], rows[:, ZF + index : ZF + index + 1])

    terms = []
    for j in range(groups):
        group = lax.rem(where[0] + groups - j, groups)
        rows = stats[group]
        rows = rows.reshape(-1, LANES)
        columns = spread_field(rows, FIELD_COUNT)
        total = jnp.sum(columns, axis=0, keepdims=True)
        for p in range(2):
            mean = spread_field(rows, 2 * p)
            square = spread_field(rows, 2 * p + 1)
            average = jnp.sum(columns * mean, axis=0, keepdims=True) / total
            off = mean - average
            square = jnp.sum(square + (zs * columns) * off * off, axis=0, keepdims=True)
            inverse = 1.0 / jnp.sqrt(square / (total * zs) + EPSILON)
            quat = [spread_field(rows[:1], FIELD_QUAT + 4 * p + c) for c in range(4)]
            terms.append((parts.at[p, j], average, inverse, quat))

    def column(y):
        at = pl.ds(pl.multiple_of(y * xs, 8), xs)
        scores = [(ref[at, :] - average) * inverse for ref, average, inverse, _ in terms]
        high = functools.reduce(jnp.maximum, scores)
        high = jnp.maximum(high, pltpu.roll(high, ZF, 1))
        weights = [jnp.exp(score - high) for score in scores]
        sums = [functools.reduce(jnp.add, weights)]
        for c in range(4):
            sums.append(functools.reduce(jnp.add, [w * t[3][c] for w, t in zip(weights, terms)]))
        return [high] + [value + pltpu.roll(value, ZF, 1) for value in sums]

    for j in range(valid.shape[1] // 2):
        both = [jnp.where(low_half, a, b) for a, b in zip(column(2 * j), column(2 * j + 1))]
        inside = jnp.where(low_half, valid[:, 2 * j : 2 * j + 1], valid[:, 2 * j + 1 : 2 * j + 2])
        inside = inside.astype(F32)
        high, total = both[0], both[1]
        lanes = slice(j * LANES, j * LANES + LANES)
        best[:, lanes] = inside * high
        evidence[:, lanes] = inside * (high + jnp.log(total))
        ratio = inside / total
        for c in range(4):
            moments[c, :, lanes] = both[2 + c] * ratio


def finished(where, valid, stats, parts, zs):
    groups = parts.shape[1]
    xs, share = valid.shape
    smem = pl.BlockSpec(memory_space=pltpu.SMEM)
    vmem = pl.BlockSpec(memory_space=pltpu.VMEM)
    flat = jax.ShapeDtypeStruct((xs, share * zs), F32)
    return pl.pallas_call(
        functools.partial(final_kernel, groups, xs, zs),
        out_shape=[flat, flat, jax.ShapeDtypeStruct((4, xs, share * zs), F32)],
        in_specs=[smem] + [vmem] * 3,
        out_specs=[vmem] * 3,
        compiler_params=pltpu.CompilerParams(vmem_limit_bytes=48 << 20),
        name="finish_scores",
    )(where, valid, stats, parts)


def local(tomogram, templates, valid, quats, rot_index):
    xs, voxels = tomogram.shape
    ys = valid.shape[1]
    zs = voxels // ys
    plan = Plan(xs, ys, zs)
    tiles, groups = lax.axis_size("tile"), lax.axis_size("rot")
    rot = lax.axis_index("rot")
    share = ys // groups
    per = templates.shape[1] // TEMPL
    block = templates.reshape(2, 2, per, TEMPL).transpose(0, 2, 1, 3)
    block = jnp.pad(block, ((0, 0), (0, BLOCK - per), (0, 0), (0, ZF - TEMPL)))
    block = block.reshape(2, BLOCK, LANES)
    columns = jnp.sum(valid).astype(F32)
    one_hot = rot_index[:, None] == jnp.arange(quats.shape[1], dtype=jnp.int32)[None, :]
    orient = jnp.sum(jnp.where(one_hot[:, None, :], quats[None], 0.0), axis=2)
    fields = orient.reshape(2, 2, 4).transpose(1, 0, 2).reshape(2, 8)
    extra = jnp.concatenate(
        [jnp.zeros((2, 4), F32), jnp.full((2, 1), columns), fields, jnp.zeros((2, ZF - 13), F32)],
        axis=1,
    ).reshape(1, LANES)
    parts, rows = matched(plan, tiles, groups, tomogram, block, valid, extra)
    own_valid = lax.dynamic_slice_in_dim(valid, rot * share, share, 1)
    where = rot.astype(jnp.int32).reshape(1)
    rows = rows.reshape(groups, tiles, 1, LANES)
    return tuple(finished(where, own_valid, rows, parts, zs))


def solution(mesh):
    placed = (P("tile", None), P("rot", "tile"), P("tile", None), P(), P("rot"))
    return jax.shard_map(
        local,
        mesh=mesh,
        in_specs=placed,
        out_specs=(P("tile", "rot"), P("tile", "rot"), P(None, "tile", "rot")),
        check_vma=False,
    )
```

time: 690 us -> 120 us (0.17)
  blocking collectives: 307 us -> 0 us
  waiting for transfers between devices: 127 us -> 0 us
  Pallas kernels: 0 us -> 109 us
  matrix products: 101 us -> 0 us
  local copies, waits for them, and re-layouts: 68.8 us -> 5.78 us
  other arithmetic: 56.8 us -> 3.29 us
  between operations: 15.1 us -> 1.34 us
    psum x2 -> x0, blocking collectives: 251 us -> none  [the longest x1 127 us: local(): lax.psum(jnp.sum(inside[None] * deviation * deviation, axis=(1, 2)), 'tile')]
    pallas_call x0 -> x2, Pallas kernels: none -> 109 us  [the longest x1 103 us: matched(): pl.pallas_call(functools.partial(match_kernel, plan, tiles, groups), out_...]
    dot_general x29 -> x0, matrix products: 101 us -> none  [product(): jnp.einsum(formula, left_arr, right_arr, precision=lax.Precision.HIGH, pr...]
    psum x1 -> x0, waiting for transfers between devices: 85.2 us -> none  [local(): lax.psum((exp_total * rescale, moment * rescale[None]), 'rot')]
    all_gather x1 -> x0, blocking collectives: 55.7 us -> none  [local(): lax.all_gather(templates, 'tile', axis=1, tiled=True).astype(jnp.float32)]
    pmax x1 -> x0, waiting for transfers between devices: 41.4 us -> none  [local(): high_full = lax.pmax(highest, 'rot')]
    transpose x5 -> x1, local copies, waits for them, and re-layouts: 27.7 us -> 0.01 us  [local(): fields = orient.reshape(2, 2, 4).transpose(1, 0, 2).reshape(2, 8)]
    sub x4 -> x0, other arithmetic: 23.7 us -> none  [multiply(): first_arr[0] * other_arr[0] - first_arr[1] * other_arr[1]]
  transfers between devices with their start and end apart: 4 -> 0, of which waited for: 2 -> 0; matrix products, arithmetic and copies ran while one was open for 2% -> 0% of each run, Pallas kernels for 0% -> 0%
where the time goes in v2:
time: 120 us; the launch traced here: 119 us
  Pallas kernels  109 us (91%)
  local copies, waits for them, and re-layouts  5.78 us (5%)
  other arithmetic  3.29 us (3%)
  between operations  1.34 us (1%)
    pallas_call x1, Pallas kernels, matched(): pl.pallas_call(functools.partial(match_kernel, plan, tiles, groups), out_...  103 us
    pallas_call x1, Pallas kernels, finished(): pl.pallas_call(functools.partial(final_kernel, groups, xs, zs), out_shape...  6.44 us
    unnamed x5, local copies, waits for them, and re-layouts  2.67 us

profile of v2, /device:TPU:1, one launch (start us, length us, event | category | flops | bytes accessed | tf_op | source)
XLA Modules:
  0.0 119.5 jit_solution(12724312683031748190)
XLA Ops:
  0.6 1.4 %reduce_sum.18 = s32[]{:T(128)} reduce(s32[32,80]{1,0:T(8,128)} %valid.1, s32[]{:T(128)} %constant.18.clone.1), dimensions={0,1}, to_apply=%region_0.1 | reduce | flops 2559 | bytes 10248 | tf_op jit(solution)/shard_map/reduce_sum | solution.py:579
  2.7 0.1 pad.8.clone
  2.7 0.1 pad_maximum_fusion
  2.8 0.8 constant_dynamic-slice_fusion.valid
  3.6 0.7 iota_compare_fusion
  4.3 1.0 select_reduce_fusion
  5.4 0.1 reshape.49
  5.5 0.1 maximum_maximum_fusion
  5.6 0.6 reshape.50.extra
  6.1 0.8 reshape.46
  7.1 0.7 reshape.47.block
  7.8 102.6 %match.1 = (f32[2,4,640,128]{3,2,1,0:T(8,128)}, f32[4,8,8,1,128]{4,3,2,1,0:T(1,128)}) custom-call(bf16[32,5120]{1,0:T(8,128)(2,1)} %own.1, bf16[2,48,128]{2,1,0:T(8,128)(2,1)} %reshape.47.block, s32[32,80]{1,0:T(8,128)} %valid.1, f32[1,128]{1,0:T(1,128)} %reshape.50.extra, bf16[256,512]{1,0:T(8,128)(2,1)} %constant.38.clone.slab_z, ...), custom_call_target="tpu_custom_call" | custom-call | tf_op jit(solution)/shard_map/match/pallas_call | solution.py:467
  110.4 0.0 copy-start
  110.4 1.7 %copy-done = f32[2,4,640,128]{3,2,1,0:T(8,128)S(1)} copy-done((f32[2,4,640,128]{3,2,1,0:T(8,128)S(1)}, f32[2,4,640,128]{3,2,1,0:T(8,128)}, u32[]{:S(2)}) %copy-start) | copy-done | bytes 2621464
  112.1 0.0 copy-start.1
  112.1 0.9 copy-done.1
  113.0 6.4 %finish_scores.1 = (f32[32,1280]{1,0:T(8,128)}, f32[32,1280]{1,0:T(8,128)}, f32[4,32,1280]{2,1,0:T(8,128)}) custom-call(s32[1]{0:T(128)} %bitcast.where, s32[32,20]{1,0:T(8,128)S(1)} %constant_dynamic-slice_fusion.valid, f32[4,64,1,128]{3,2,1,0:T(1,128)S(1)} %bitcast.7, f32[2,4,640,128]{3,2,1,0:T(8,128)S(1)} %copy-done), custom_call_target="tpu_custom_call" | custom-call | tf_op jit(solution)/shard_map/finish_scores/pallas_call | solution.py:557
  (5 shorter events, 0.1 us)
Async XLA Ops:
  110.4 1.7 %copy-start = (f32[2,4,640,128]{3,2,1,0:T(8,128)S(1)}, f32[2,4,640,128]{3,2,1,0:T(8,128)}, u32[]{:S(2)}) copy-start(f32[2,4,640,128]{3,2,1,0:T(8,128)} %get-tuple-element.6.parts) | copy-start | bytes 7864324
  112.1 0.9 copy-start.1

commit v3 on v2

--- a/solution.py
+++ b/solution.py
@@ -17,7 +17,8 @@
 ZF = 64
 CORES = 2
 RING_X = 4
-BLOCK = 48
+BLOCK = 80
+HALO_PARTS = 4
 MESH = pl.DeviceIdType.MESH
 FIELD_COUNT = 4
 FIELD_QUAT = 5
@@ -77,10 +78,8 @@
         angle = phases(np.arange(self.zs), np.arange(self.kz), self.lz)
         cos = padded_cols(np.cos(angle), ZF)
         sin = padded_cols(-np.sin(angle), ZF)
-        one = np.concatenate([cos, cos, sin, sin], axis=1)
-        none = np.zeros_like(one)
-        high, low = halves(np.block([[one, none], [none, one]]))
-        return np.concatenate([high, low], axis=0)
+        one = np.concatenate([cos, sin], axis=1)
+        return np.kron(np.eye(2), one)
 
     def tmpl_z(self):
         angle = phases(np.arange(TEMPL) - HALF, np.arange(self.kz), self.lz)
@@ -209,10 +208,18 @@
         copy.wait()
 
 
+def packed_sides(folded, count, low_half):
+    cos, sin = folded[:count], folded[count:]
+    swapped = pltpu.roll(sin, ZF, 1)
+    turned = jnp.where(low_half, swapped, -swapped)
+    return cos + turned, cos - turned
+
+
 def match_kernel(
-    plan, tiles, groups, own, block, valid, extra, slab_z, slab_x, slab_y, table_z, table_x,
-    table_y, table_yi, table_xi, table_zi, zsum, ones, parts, stats, low, high, bank, spectrum,
-    slab_mid, zed, mid, back, marks, ready, row, sends, receives, part_sends, part_receives,
+    plan, tiles, groups, own, block, valid, quats, rot_index, slab_z, slab_x, slab_y, table_z,
+    table_x, table_y, table_yi, table_xi, table_zi, zsum, ones, best, evidence, moments, parts,
+    stats, low, high, bank, spectrum, slab_mid, zed, mid, back, marks, ready, row, sends,
+    receives, part_sends, part_receives,
 ):
     ring_z = tiles // (CORES * RING_X)
     plane_size = RING_X * CORES
@@ -225,7 +232,7 @@
     flat = x * CORES + core
     z_peers = [{"tile": tile_of(lax.rem(z + d, ring_z), x, core)} for d in range(1, ring_z)]
     x_peers = [{"tile": tile_of(z, lax.rem(x + d, RING_X), core)} for d in range(1, RING_X)]
-    other = [{"tile": tile_of(z, x, 1 - core)}]
+    other = {"tile": tile_of(z, x, 1 - core)}
     plane = []
     for d in range(1, plane_size):
         there = lax.rem(flat + d, plane_size)
@@ -233,24 +240,43 @@
     rot_peers = [{"rot": lax.rem(rot + d, groups)} for d in range(1, groups)]
     after = {"tile": lax.rem(tile + 1, tiles)}
     before = {"tile": lax.rem(tile + tiles - 1, tiles)}
-
+    low_half = lax.broadcasted_iota(jnp.int32, (1, LANES), 1) < ZF
+    width = ys * plan.zs // HALO_PARTS
+    first_halo, first_z = 0, 2 * HALO_PARTS
+    first_x = first_z + ring_z - 1
+    first_pass = first_x + RING_X
+    first_stats = first_pass + RING_X - 1
+
+    greet([after, before] + z_peers + plane + rot_peers)
+
+    def halo(q):
+        lanes = pl.ds(pl.multiple_of(q * width, LANES), width)
+        return [
+            remote(own.at[:, lanes], low.at[:, lanes], sends, receives, first_halo + 2 * q, after),
+            remote(own.at[:, lanes], high.at[:, lanes], sends, receives, first_halo + 2 * q + 1, before),
+        ]
+
+    for q in range(HALO_PARTS):
+        for copy in halo(q):
+            copy.start()
     bank[core, x, z] = block[...]
-    greet([after, before] + z_peers + plane + rot_peers)
-    halo = [
-        remote(own, low, sends, receives, 0, after),
-        remote(own, high, sends, receives, 1, before),
-    ]
-    for copy in halo:
-        copy.start()
     mine = bank.at[core, x, z]
-    copies = begin(mine, mine, sends, receives, 2, z_peers)
+    copies = begin(mine, mine, sends, receives, first_z, z_peers)
 
     flags = valid[...].astype(F32)
     columns = jnp.sum(flags)
     for y in range(ys):
         marks[y * xs : y * xs + xs, :] = jnp.broadcast_to(flags[:, y : y + 1], (xs, LANES))
-    row[...] = extra[...]
-    finish(halo)
+    field = lax.rem(lax.broadcasted_iota(jnp.int32, (1, LANES), 1), ZF)
+    line = jnp.where(field == FIELD_COUNT, columns, 0.0)
+    entry = lax.broadcasted_iota(jnp.int32, quats.shape, 1)
+    for r in range(4):
+        found = jnp.sum(jnp.where(entry == rot_index[r], quats[...], 0.0), axis=1, keepdims=True)
+        half = low_half if r % 2 == 0 else jnp.logical_not(low_half)
+        for c in range(4):
+            here = jnp.logical_and(field == FIELD_QUAT + 4 * (r // 2) + c, half)
+            line = jnp.where(here, found[c : c + 1], line)
+    row[...] = line
 
     def slab_first(j, carry):
         lanes = pl.ds(pl.multiple_of(j * LANES, LANES), LANES)
@@ -261,84 +287,117 @@
         ]
         strip = jnp.concatenate(strips, axis=0).astype(BF16)
         strip = mm(jnp.concatenate([strip, strip], axis=1), slab_z[...])
+        folded = stacked_product(slab_x[...], strip)
         for part in range(2):
-            folded = stacked_product(slab_x[...], strip[:, part * 256 : part * 256 + 256])
-            for s, (re, im) in enumerate(plus_minus(folded, kxp, -1)):
+            sides = packed_sides(folded[:, part * LANES : part * LANES + LANES], kxp, low_half)
+            for s in range(2):
                 at = pl.ds(pl.multiple_of((2 * j + part) * rows + s * kxp, 8), kxp)
-                slab_mid[0, at, :] = re
-                slab_mid[1, at, :] = im
+                slab_mid[at, :] = sides[s]
         return carry
 
-    trips = ys // 2 // 4
-    lax.fori_loop(0, trips // 2, unrolled(slab_first, 4), 0)
+    pieces = ys // 2 // HALO_PARTS
+
+    def slab_part(q, carry):
+        for copy in halo(q):
+            copy.wait()
+
+        def body(i, inner):
+            return lax.fori_loop(
+                0, 5, lambda t, c: slab_first(q * pieces + i * 5 + t, c), inner, unroll=True
+            )
+
+        return lax.fori_loop(0, pieces // 5, body, carry)
+
+    lax.fori_loop(0, HALO_PARTS // 2, slab_part, 0)
     finish(copies)
     mine = bank.at[core, x]
-    copies = begin(mine, mine, sends, receives, 1 + ring_z, x_peers)
-    lax.fori_loop(trips // 2, trips, unrolled(slab_first, 4), 0)
-    finish(copies)
-    mine = bank.at[core]
-    copies = begin(mine, mine, sends, receives, ring_z + RING_X, other)
+    copies = begin(mine, mine, sends, receives, first_x, x_peers + [other])
+    lax.fori_loop(HALO_PARTS // 2, HALO_PARTS, slab_part, 0)
 
     def slab_second(k, carry):
+        lines = [slab_mid[pl.ds(k + s * kxp, ys, stride=rows), :] for s in range(2)]
+        folded = stacked_product(slab_y[...], jnp.concatenate(lines, axis=1))
         for s in range(2):
-            at = pl.ds(k + s * kxp, ys, stride=rows)
-            value = jnp.concatenate([slab_mid[0, at, :], slab_mid[1, at, :]], axis=1)
-            folded = stacked_product(slab_y[...], value)
-            for u, (re, im) in enumerate(plus_minus(folded, kyp, -1)):
-                spectrum[k, s, u, :, :LANES] = re
-                spectrum[k, s, u, :, LANES:] = im
+            sides = packed_sides(folded[:, s * LANES : s * LANES + LANES], kyp, low_half)
+            for u in range(2):
+                swapped = pltpu.roll(sides[u], ZF, 1)
+                spectrum[k, s, u, :, :LANES] = jnp.where(low_half, sides[u], swapped)
+                spectrum[k, s, u, :, LANES:] = jnp.where(low_half, swapped, sides[u])
         return carry
 
-    lax.fori_loop(0, plan.kxc // 11, unrolled(slab_second, 11), 0)
-    finish(copies)
+    trips = plan.kxc // 11
+    lax.fori_loop(0, trips // 2, unrolled(slab_second, 11), 0)
+    forwards = []
+    for d in range(1, RING_X):
+        copies[d - 1].wait()
+        mine = bank.at[core, lax.rem(x + RING_X - d, RING_X)]
+        forward = remote(mine, mine, sends, receives, first_pass + d - 1, other)
+        forward.start()
+        forwards.append(forward)
+    lax.fori_loop(trips // 2, trips, unrolled(slab_second, 11), 0)
+    copies[-1].wait()
+    finish(forwards)
 
     per = TEMPL * TEMPL // tiles
     total = float(TEMPL**3)
     lane = lax.broadcasted_iota(jnp.int32, (BLOCK, LANES), 1)
-    line = lax.broadcasted_iota(jnp.int32, (BLOCK, LANES), 0)
-    used = jnp.logical_and(lax.rem(lane, ZF) < TEMPL, line < per)[None]
-    field = lax.rem(lax.broadcasted_iota(jnp.int32, (1, LANES), 1), ZF)
+    place = lax.broadcasted_iota(jnp.int32, (BLOCK, LANES), 0)
+    used = jnp.logical_and(lax.rem(lane, ZF) < TEMPL, place < 2 * per)[None]
+    tall = ring_z * BLOCK
+
+    def lane_groups(value):
+        wide = jnp.broadcast_to(jnp.sum(value, axis=0, keepdims=True), (8, LANES))
+        return exact(wide, ones[...])[:1]
+
+    def both_pairs(value):
+        first = lane_groups(jnp.where(place < per, value, 0.0))
+        second = lane_groups(jnp.where(place < per, 0.0, value))
+        return first, second
+
+    def bank_rows(i):
+        return bank[i // RING_X, lax.rem(i, RING_X)]
+
+    def add_up(i, carry):
+        return carry + jnp.sum(bank_rows(i).astype(F32), axis=0)
+
+    empty = jnp.zeros((BLOCK, LANES), F32)
+    means = both_pairs(lax.fori_loop(0, plane_size, add_up, empty))
+    means = [mean / total for mean in means]
+    mean_rows = jnp.where(place < per, means[0], means[1])[None]
+
+    def add_squares(i, carry):
+        off = jnp.where(used, bank_rows(i).astype(F32) - mean_rows, 0.0)
+        return carry + jnp.sum(off * off, axis=0)
+
+    squares = both_pairs(lax.fori_loop(0, plane_size, add_squares, empty))
+    factors = [
+        1.0 / (jnp.sqrt(square / total + EPSILON) * float(TEMPL) ** 1.5) for square in squares
+    ]
+    scale_rows = jnp.where(place < per, factors[0], factors[1])[None]
+
+    def z_stage(i, carry):
+        lines = bank_rows(i).reshape(tall, LANES)
+        value = mm(jnp.concatenate([lines, lines], axis=1), table_z[...])
+        at = pl.ds(pl.multiple_of(i * tall, tall), tall)
+        for part in range(2):
+            lanes = slice(part * LANES, part * LANES + LANES)
+            side = value[:, lanes].reshape(ring_z, BLOCK, LANES)
+            side = (side - mean_rows * zsum[:, lanes]) * scale_rows
+            zed[part, at, :] = side.reshape(tall, LANES)
+        return carry
+
+    lax.fori_loop(0, plane_size, z_stage, 0)
     share = ys // groups
     step = share
-    tall = ring_z * BLOCK
 
     def pair(p, outer):
-        def add_up(i, carry):
-            value = bank[i // RING_X, lax.rem(i, RING_X), :, p].astype(F32)
-            return carry + tall_sum(value.reshape(tall, LANES))
-
-        sums = lax.fori_loop(0, plane_size, add_up, jnp.zeros((8, LANES), F32))
-        mean = jnp.sum(exact(sums, ones[...]), axis=0, keepdims=True) / total
-
-        def add_squares(i, carry):
-            value = bank[i // RING_X, lax.rem(i, RING_X), :, p].astype(F32)
-            off = jnp.where(used, value - mean[None], 0.0)
-            return carry + tall_sum((off * off).reshape(tall, LANES))
-
-        squares = lax.fori_loop(0, plane_size, add_squares, jnp.zeros((8, LANES), F32))
-        variance = jnp.sum(exact(squares, ones[...]), axis=0, keepdims=True) / total
-        factor = 1.0 / (jnp.sqrt(variance + EPSILON) * float(TEMPL) ** 1.5)
-        shift = jnp.concatenate([mean, mean], axis=1) * zsum[...]
-        scale = jnp.concatenate([factor, factor], axis=1)
-
-        def z_stage(i, carry):
-            lines = bank[i // RING_X, lax.rem(i, RING_X), :, p].reshape(tall, LANES)
-            value = mm(jnp.concatenate([lines, lines], axis=1), table_z[...])
-            value = (value - shift) * scale
-            at = pl.ds(pl.multiple_of(i * tall, tall), tall)
-            zed[0, at, :] = value[:, :LANES]
-            zed[1, at, :] = value[:, LANES:]
-            return carry
-
-        lax.fori_loop(0, plane_size, z_stage, 0)
-
         def x_stage(b, carry):
             lines = []
             for s in range(TEMPL // ring_z):
                 index = s * TEMPL + b
                 owner = index // per
                 there = lax.rem(owner, CORES) * RING_X + owner // CORES
-                at = pl.ds(there * tall + lax.rem(index, per), ring_z, stride=BLOCK)
+                at = pl.ds(there * tall + p * per + lax.rem(index, per), ring_z, stride=BLOCK)
                 lines.append(jnp.concatenate([zed[0, at, :], zed[1, at, :]], axis=1))
             folded = stacked_product(table_x[...], jnp.concatenate(lines, axis=0))
             for s, (re, im) in enumerate(plus_minus(folded, kxp, 1)):
@@ -377,7 +436,7 @@
         lax.fori_loop(0, plan.kxc // 11, unrolled(y_stage, 11), 0)
 
         def last(i, lane_sum):
-            j = lax.rem(i + 1, groups)
+            j = lax.rem(2 + 3 * i + 3 * (i * (i - 1) // 2), groups)
             base = lax.rem(rot + j, groups) * share
             lines = []
             for y in range(step):
@@ -428,28 +487,78 @@
 
     lax.fori_loop(0, 2, pair, 0)
     stats[rot, flat, z] = row[...]
-    first = 1 + ring_z + RING_X
     mine = stats.at[rot, flat, z]
-    finish(begin(mine, mine, sends, receives, first, z_peers))
+    finish(begin(mine, mine, sends, receives, first_stats, z_peers))
     mine = stats.at[rot, flat]
-    finish(begin(mine, mine, sends, receives, first + ring_z - 1, plane))
+    finish(begin(mine, mine, sends, receives, first_stats + ring_z - 1, plane))
     mine = stats.at[rot]
-    finish(begin(mine, mine, sends, receives, first + ring_z + plane_size - 2, rot_peers))
-    for p in range(2):
-        for j in range(1, groups):
-            remote(
-                ready.at[p, j], parts.at[p, j], part_sends.at[p], part_receives.at[p], j, rot_peers[j - 1]
-            ).wait()
-
-
-def matched(plan, tiles, groups, own, block, valid, extra):
+    finish(begin(mine, mine, sends, receives, first_stats + ring_z + plane_size - 2, rot_peers))
+    incoming = [
+        remote(ready.at[p, j], parts.at[p, j], part_sends.at[p], part_receives.at[p], j, rot_peers[j - 1])
+        for p in range(2)
+        for j in range(1, groups)
+    ]
+
+    def spread_field(lines, index):
+        return jnp.where(
+            low_half, lines[:, index : index + 1], lines[:, ZF + index : ZF + index + 1]
+        )
+
+    terms = []
+    for j in range(groups):
+        group = lax.rem(rot + groups - j, groups)
+        lines = stats[group].reshape(-1, LANES)
+        count = spread_field(lines, FIELD_COUNT)
+        total = jnp.sum(count, axis=0, keepdims=True)
+        for p in range(2):
+            mean = spread_field(lines, 2 * p)
+            square = spread_field(lines, 2 * p + 1)
+            average = jnp.sum(count * mean, axis=0, keepdims=True) / total
+            off = mean - average
+            square = jnp.sum(square + (plan.zs * count) * off * off, axis=0, keepdims=True)
+            inverse = 1.0 / jnp.sqrt(square / (total * plan.zs) + EPSILON)
+            quat = [spread_field(lines[:1], FIELD_QUAT + 4 * p + c) for c in range(4)]
+            terms.append((parts.at[p, j], average, inverse, quat))
+
+    finish(incoming)
+
+    def column(y):
+        at = pl.ds(pl.multiple_of(y * xs, 8), xs)
+        scores = [(ref[at, :] - average) * inverse for ref, average, inverse, _ in terms]
+        high = functools.reduce(jnp.maximum, scores)
+        high = jnp.maximum(high, pltpu.roll(high, ZF, 1))
+        weights = [jnp.exp(score - high) for score in scores]
+        sums = [functools.reduce(jnp.add, weights)]
+        for c in range(4):
+            sums.append(functools.reduce(jnp.add, [w * t[3][c] for w, t in zip(weights, terms)]))
+        return [high] + [value + pltpu.roll(value, ZF, 1) for value in sums]
+
+    def answer(j, carry):
+        both = [jnp.where(low_half, a, b) for a, b in zip(column(2 * j), column(2 * j + 1))]
+        base = pl.multiple_of(rot * (share * xs) + 2 * j * xs, 8)
+        inside = jnp.where(
+            low_half, marks[pl.ds(base, xs), :], marks[pl.ds(pl.multiple_of(base + xs, 8), xs), :]
+        )
+        high, total = both[0], both[1]
+        lanes = pl.ds(pl.multiple_of(j * LANES, LANES), LANES)
+        best[:, lanes] = inside * high
+        evidence[:, lanes] = inside * (high + jnp.log(total))
+        ratio = inside / total
+        for c in range(4):
+            moments[c, :, lanes] = both[2 + c] * ratio
+        return carry
+
+    lax.fori_loop(0, share // 2 // 5, unrolled(answer, 5), 0)
+
+
+def matched(plan, tiles, groups, own, block, valid, quats, rot_index):
     ring_z = tiles // (CORES * RING_X)
     order = (
         np.arange(TEMPL // ring_z)[:, None] + (TEMPL // ring_z) * np.arange(ring_z)[None]
     ).reshape(-1)
     z_table = plan.tmpl_z()
     tables = [
-        plan.slab_z(),
+        row_stack(plan.slab_z()),
         stacked_table(plan.folded(plan.kx, plan.kxp, np.arange(plan.lx), plan.lx)),
         stacked_table(plan.folded(plan.ky, plan.kyp, np.arange(plan.ys), plan.ly)),
         row_stack(z_table),
@@ -462,22 +571,24 @@
         np.kron(np.eye(2), np.ones((ZF, ZF))).astype(np.float32),
     ]
     share = plan.ys // groups * plan.xs
-    copies = ring_z + RING_X + 1 + ring_z + RING_X * CORES + groups - 3
+    copies = 2 * HALO_PARTS + 2 * ring_z + 2 * RING_X + RING_X * CORES + groups - 5
     vmem = pl.BlockSpec(memory_space=pltpu.VMEM)
+    flat_out = jax.ShapeDtypeStruct((plan.xs, plan.ys // groups * plan.zs), F32)
     return pl.pallas_call(
         functools.partial(match_kernel, plan, tiles, groups),
-        out_shape=[
-            jax.ShapeDtypeStruct((2, groups, share, LANES), F32),
-            jax.ShapeDtypeStruct((groups, RING_X * CORES, ring_z, 1, LANES), F32),
-        ],
-        in_specs=[vmem] * (4 + len(tables)),
-        out_specs=[vmem] * 2,
+        out_shape=[flat_out, flat_out, jax.ShapeDtypeStruct((4,) + flat_out.shape, F32)],
+        in_specs=[vmem] * 4
+        + [pl.BlockSpec(memory_space=pltpu.SMEM)]
+        + [vmem] * len(tables),
+        out_specs=[vmem] * 3,
         scratch_shapes=[
+            pltpu.VMEM((2, groups, share, LANES), F32),
+            pltpu.VMEM((groups, RING_X * CORES, ring_z, 1, LANES), F32),
             pltpu.VMEM(own.shape, BF16),
             pltpu.VMEM(own.shape, BF16),
             pltpu.VMEM((CORES, RING_X, ring_z) + block.shape, BF16),
             pltpu.VMEM((plan.kxc, 2, 2, plan.kyp, 2 * LANES), F32),
-            pltpu.VMEM((2, plan.ys * 2 * plan.kxp, LANES), F32),
+            pltpu.VMEM((plan.ys * 2 * plan.kxp, LANES), F32),
             pltpu.VMEM((2, tiles * BLOCK, LANES), F32),
             pltpu.VMEM((2, TEMPL * 2 * plan.kxp, LANES), F32),
             pltpu.VMEM((2, plan.kxi * plan.ys, LANES), F32),
@@ -493,75 +604,11 @@
             collective_id=0, has_side_effects=True, vmem_limit_bytes=60 << 20
         ),
         name="match",
-    )(own, block, valid, extra, *tables)
+    )(own, block, valid, quats, rot_index, *tables)
 
 
 def row_stack(table):
     return np.concatenate(halves(table), axis=0)
-
-
-def final_kernel(groups, xs, zs, where, valid, stats, parts, best, evidence, moments):
-    lane = lax.broadcasted_iota(jnp.int32, (1, LANES), 1)
-    low_half = lane < ZF
-
-    def spread_field(rows, index):
-        return jnp.where(low_half, rows[:, index : index + 1], rows[:, ZF + index : ZF + index + 1])
-
-    terms = []
-    for j in range(groups):
-        group = lax.rem(where[0] + groups - j, groups)
-        rows = stats[group]
-        rows = rows.reshape(-1, LANES)
-        columns = spread_field(rows, FIELD_COUNT)
-        total = jnp.sum(columns, axis=0, keepdims=True)
-        for p in range(2):
-            mean = spread_field(rows, 2 * p)
-            square = spread_field(rows, 2 * p + 1)
-            average = jnp.sum(columns * mean, axis=0, keepdims=True) / total
-            off = mean - average
-            square = jnp.sum(square + (zs * columns) * off * off, axis=0, keepdims=True)
-            inverse = 1.0 / jnp.sqrt(square / (total * zs) + EPSILON)
-            quat = [spread_field(rows[:1], FIELD_QUAT + 4 * p + c) for c in range(4)]
-            terms.append((parts.at[p, j], average, inverse, quat))
-
-    def column(y):
-        at = pl.ds(pl.multiple_of(y * xs, 8), xs)
-        scores = [(ref[at, :] - average) * inverse for ref, average, inverse, _ in terms]
-        high = functools.reduce(jnp.maximum, scores)
-        high = jnp.maximum(high, pltpu.roll(high, ZF, 1))
-        weights = [jnp.exp(score - high) for score in scores]
-        sums = [functools.reduce(jnp.add, weights)]
-        for c in range(4):
-            sums.append(functools.reduce(jnp.add, [w * t[3][c] for w, t in zip(weights, terms)]))
-        return [high] + [value + pltpu.roll(value, ZF, 1) for value in sums]
-
-    for j in range(valid.shape[1] // 2):
-        both = [jnp.where(low_half, a, b) for a, b in zip(column(2 * j), column(2 * j + 1))]
-        inside = jnp.where(low_half, valid[:, 2 * j : 2 * j + 1], valid[:, 2 * j + 1 : 2 * j + 2])
-        inside = inside.astype(F32)
-        high, total = both[0], both[1]
-        lanes = slice(j * LANES, j * LANES + LANES)
-        best[:, lanes] = inside * high
-        evidence[:, lanes] = inside * (high + jnp.log(total))
-        ratio = inside / total
-        for c in range(4):
-            moments[c, :, lanes] = both[2 + c] * ratio
-
-
-def finished(where, valid, stats, parts, zs):
-    groups = parts.shape[1]
-    xs, share = valid.shape
-    smem = pl.BlockSpec(memory_space=pltpu.SMEM)
-    vmem = pl.BlockSpec(memory_space=pltpu.VMEM)
-    flat = jax.ShapeDtypeStruct((xs, share * zs), F32)
-    return pl.pallas_call(
-        functools.partial(final_kernel, groups, xs, zs),
-        out_shape=[flat, flat, jax.ShapeDtypeStruct((4, xs, share * zs), F32)],
-        in_specs=[smem] + [vmem] * 3,
-        out_specs=[vmem] * 3,
-        compiler_params=pltpu.CompilerParams(vmem_limit_bytes=48 << 20),
-        name="finish_scores",
-    )(where, valid, stats, parts)
 
 
 def local(tomogram, templates, valid, quats, rot_index):
@@ -570,25 +617,11 @@
     zs = voxels // ys
     plan = Plan(xs, ys, zs)
     tiles, groups = lax.axis_size("tile"), lax.axis_size("rot")
-    rot = lax.axis_index("rot")
-    share = ys // groups
     per = templates.shape[1] // TEMPL
     block = templates.reshape(2, 2, per, TEMPL).transpose(0, 2, 1, 3)
-    block = jnp.pad(block, ((0, 0), (0, BLOCK - per), (0, 0), (0, ZF - TEMPL)))
-    block = block.reshape(2, BLOCK, LANES)
-    columns = jnp.sum(valid).astype(F32)
-    one_hot = rot_index[:, None] == jnp.arange(quats.shape[1], dtype=jnp.int32)[None, :]
-    orient = jnp.sum(jnp.where(one_hot[:, None, :], quats[None], 0.0), axis=2)
-    fields = orient.reshape(2, 2, 4).transpose(1, 0, 2).reshape(2, 8)
-    extra = jnp.concatenate(
-        [jnp.zeros((2, 4), F32), jnp.full((2, 1), columns), fields, jnp.zeros((2, ZF - 13), F32)],
-        axis=1,
-    ).reshape(1, LANES)
-    parts, rows = matched(plan, tiles, groups, tomogram, block, valid, extra)
-    own_valid = lax.dynamic_slice_in_dim(valid, rot * share, share, 1)
-    where = rot.astype(jnp.int32).reshape(1)
-    rows = rows.reshape(groups, tiles, 1, LANES)
-    return tuple(finished(where, own_valid, rows, parts, zs))
+    block = jnp.pad(block, ((0, 0), (0, 0), (0, 0), (0, ZF - TEMPL))).reshape(2 * per, LANES)
+    block = jnp.pad(block, ((0, BLOCK - 2 * per), (0, 0)))
+    return tuple(matched(plan, tiles, groups, tomogram, block, valid, quats, rot_index))
 
 
 def solution(mesh):

time: 120 us -> 104 us (0.87)
  Pallas kernels: 109 us -> 97.4 us
  other arithmetic: 3.29 us -> 0 us
    pallas_call x1 -> x0, Pallas kernels: 6.44 us -> none  [finished(): pl.pallas_call(functools.partial(final_kernel, groups, xs, zs), out_shape...]
    pallas_call x1, Pallas kernels: 103 us -> 97.4 us  [matched(): pl.pallas_call(functools.partial(match_kernel, plan, tiles, groups), out_...]
    reduce_sum x2 -> x0, other arithmetic: 2.39 us -> none  [the longest x1 1.36 us: local(): columns = jnp.sum(valid).astype(F32)]
    unnamed x5 -> x6, local copies, waits for them, and re-layouts: 2.67 us -> 4.12 us
    reshape x3 -> x1, local copies, waits for them, and re-layouts: 1.38 us -> 0.09 us  [local(): jnp.pad(block, ((0, 0), (0, 0), (0, 0), (0, ZF - TEMPL)))]
where the time goes in v3:
time: 104 us
  Pallas kernels  97.4 us (94%)
  local copies, waits for them, and re-layouts  5.68 us (5%)
    pallas_call x1, Pallas kernels, matched(): pl.pallas_call(functools.partial(match_kernel, plan, tiles, groups), out_...  97.4 us
    unnamed x6, local copies, waits for them, and re-layouts  4.12 us

profile of v3, /device:TPU:1, one launch (start us, length us, event | category | flops | bytes accessed | tf_op | source)
XLA Modules:
  0.0 103.7 jit_solution(13723265992428077268)
XLA Ops:
  0.6 0.8 reshape.12
  1.5 0.1 reshape.13
  1.6 0.6 pad.9.block
  2.2 97.4 %match.1 = (f32[32,1280]{1,0:T(8,128)}, f32[32,1280]{1,0:T(8,128)}, f32[4,32,1280]{2,1,0:T(8,128)}) custom-call(bf16[32,5120]{1,0:T(8,128)(2,1)} %own.1, bf16[80,128]{1,0:T(8,128)(2,1)} %pad.9.block, s32[32,80]{1,0:T(8,128)} %valid.1, f32[4,4096]{1,0:T(4,128)} %quats.1, s32[4]{0:T(128)} %rot_index.1, bf16[256,256]{1,0:T(8,128)(2,1)} %constant.25.clone.slab_z, ...), custom_call_target="tpu_custom_call" | custom-call | tf_op jit(solution)/shard_map/match/pallas_call | solution.py:577
  99.6 0.0 copy-start
  99.6 1.7 %copy.25 = f32[32,1280]{1,0:T(8,128)} copy(f32[32,1280]{1,0:T(8,128)} %get-tuple-element.6) | data formatting | bytes 327680
  101.3 1.6 %copy.26 = f32[32,1280]{1,0:T(8,128)} copy(f32[32,1280]{1,0:T(8,128)} %get-tuple-element.7) | data formatting | bytes 327680
  102.9 0.0 copy-done
  102.9 0.8 copy.27
  (2 shorter events, 0.1 us)
Async XLA Ops:
  99.6 3.3 %copy-start = (f32[4,32,1280]{2,1,0:T(8,128)S(1)}, f32[4,32,1280]{2,1,0:T(8,128)}, u32[]{:S(2)}) copy-start(f32[4,32,1280]{2,1,0:T(8,128)} %get-tuple-element.8) | copy-start | bytes 1966084

commit v4 on v3

--- a/solution.py
+++ b/solution.py
@@ -216,11 +216,13 @@
 
 
 def match_kernel(
-    plan, tiles, groups, own, block, valid, quats, rot_index, slab_z, slab_x, slab_y, table_z,
-    table_x, table_y, table_yi, table_xi, table_zi, zsum, ones, best, evidence, moments, parts,
+    plan, tiles, groups, spots, own, block, valid, quats, rot_index, packed, zsum, ones, best, evidence, moments, parts,
     stats, low, high, bank, spectrum, slab_mid, zed, mid, back, marks, ready, row, sends,
     receives, part_sends, part_receives,
 ):
+    slab_z, slab_x, slab_y, table_z, table_x, table_y, table_yi, table_xi, table_zi = [
+        packed.at[first : first + tall, :wide] for first, tall, wide in spots
+    ]
     ring_z = tiles // (CORES * RING_X)
     plane_size = RING_X * CORES
     kxp, kyp, ys, xs = plan.kxp, plan.kyp, plan.ys, plan.xs
@@ -229,15 +231,19 @@
     core = lax.rem(tile, CORES)
     x = lax.rem(tile // CORES, RING_X)
     z = tile // (CORES * RING_X)
-    flat = x * CORES + core
     z_peers = [{"tile": tile_of(lax.rem(z + d, ring_z), x, core)} for d in range(1, ring_z)]
     x_peers = [{"tile": tile_of(z, lax.rem(x + d, RING_X), core)} for d in range(1, RING_X)]
     other = {"tile": tile_of(z, x, 1 - core)}
-    plane = []
-    for d in range(1, plane_size):
-        there = lax.rem(flat + d, plane_size)
-        plane.append({"tile": tile_of(z, there // CORES, lax.rem(there, CORES))})
-    rot_peers = [{"rot": lax.rem(rot + d, groups)} for d in range(1, groups)]
+    line_size, sheet_size = ring_z * CORES, RING_X * groups
+    line_peers, sheet_peers = [], []
+    for d in range(1, line_size):
+        there = lax.rem(z * CORES + core + d, line_size)
+        line_peers.append({"tile": tile_of(there // CORES, x, lax.rem(there, CORES))})
+    for d in range(1, sheet_size):
+        there = lax.rem(x * groups + rot + d, sheet_size)
+        sheet_peers.append(
+            {"tile": tile_of(z, there // groups, core), "rot": lax.rem(there, groups)}
+        )
     after = {"tile": lax.rem(tile + 1, tiles)}
     before = {"tile": lax.rem(tile + tiles - 1, tiles)}
     low_half = lax.broadcasted_iota(jnp.int32, (1, LANES), 1) < ZF
@@ -247,7 +253,7 @@
     first_pass = first_x + RING_X
     first_stats = first_pass + RING_X - 1
 
-    greet([after, before] + z_peers + plane + rot_peers)
+    greet([after, before] + line_peers + sheet_peers)
 
     def halo(q):
         lanes = pl.ds(pl.multiple_of(q * width, LANES), width)
@@ -466,7 +472,6 @@
             )
 
         lane_sum = lax.fori_loop(0, groups, last, jnp.zeros((8, LANES), F32))
-        parts[p, 0] = ready[p, 0]
         lane_mean = jnp.sum(lane_sum, axis=0, keepdims=True) / jnp.maximum(columns, 1.0)
 
         def add_off(j, carry):
@@ -486,15 +491,14 @@
         return outer
 
     lax.fori_loop(0, 2, pair, 0)
-    stats[rot, flat, z] = row[...]
-    mine = stats.at[rot, flat, z]
-    finish(begin(mine, mine, sends, receives, first_stats, z_peers))
-    mine = stats.at[rot, flat]
-    finish(begin(mine, mine, sends, receives, first_stats + ring_z - 1, plane))
-    mine = stats.at[rot]
-    finish(begin(mine, mine, sends, receives, first_stats + ring_z + plane_size - 2, rot_peers))
+    place = z * CORES + core
+    stats[rot, x, place] = row[...]
+    mine = stats.at[rot, x, place]
+    finish(begin(mine, mine, sends, receives, first_stats, line_peers))
+    mine = stats.at[rot, x]
+    finish(begin(mine, mine, sends, receives, first_stats + line_size - 1, sheet_peers))
     incoming = [
-        remote(ready.at[p, j], parts.at[p, j], part_sends.at[p], part_receives.at[p], j, rot_peers[j - 1])
+        remote(ready.at[p, j], parts.at[p, j], part_sends.at[p], part_receives.at[p], j, {"rot": lax.rem(rot + j, groups)})
         for p in range(2)
         for j in range(1, groups)
     ]
@@ -508,17 +512,19 @@
     for j in range(groups):
         group = lax.rem(rot + groups - j, groups)
         lines = stats[group].reshape(-1, LANES)
-        count = spread_field(lines, FIELD_COUNT)
+        count = lines[:, FIELD_COUNT : FIELD_COUNT + 1]
         total = jnp.sum(count, axis=0, keepdims=True)
+        average = jnp.sum(count * lines, axis=0, keepdims=True) / total
+        off = lines - average
+        square = jnp.sum(count * off * off, axis=0, keepdims=True) * plan.zs
+        square += pltpu.roll(jnp.sum(lines, axis=0, keepdims=True), LANES - 1, 1)
+        inverse = 1.0 / jnp.sqrt(square / (total * plan.zs) + EPSILON)
         for p in range(2):
-            mean = spread_field(lines, 2 * p)
-            square = spread_field(lines, 2 * p + 1)
-            average = jnp.sum(count * mean, axis=0, keepdims=True) / total
-            off = mean - average
-            square = jnp.sum(square + (plan.zs * count) * off * off, axis=0, keepdims=True)
-            inverse = 1.0 / jnp.sqrt(square / (total * plan.zs) + EPSILON)
+            source = ready if j == 0 else parts
             quat = [spread_field(lines[:1], FIELD_QUAT + 4 * p + c) for c in range(4)]
-            terms.append((parts.at[p, j], average, inverse, quat))
+            terms.append(
+                (source.at[p, j], spread_field(average, 2 * p), spread_field(inverse, 2 * p), quat)
+            )
 
     finish(incoming)
 
@@ -567,15 +573,22 @@
         paired_table(plan.inverse_rows(np.arange(plan.ys), plan.ky, plan.ly, plan.kyp, 2 * plan.kyp)),
         row_tables(plan.inverse_rows(np.arange(plan.xs), plan.kx, plan.lx, plan.kxc, plan.kxi)),
         col_tables(plan.inverse_z()),
+    ]
+    spots, first = [], 0
+    for table in tables:
+        spots.append((first, table.shape[0], table.shape[1]))
+        first += table.shape[0]
+    tables = [
+        np.concatenate([padded_cols(table, 2 * LANES) for table in tables], axis=0),
         z_table.sum(axis=0, keepdims=True).astype(np.float32),
         np.kron(np.eye(2), np.ones((ZF, ZF))).astype(np.float32),
     ]
     share = plan.ys // groups * plan.xs
-    copies = 2 * HALO_PARTS + 2 * ring_z + 2 * RING_X + RING_X * CORES + groups - 5
+    copies = 2 * HALO_PARTS + ring_z + 2 * RING_X - 2 + ring_z * CORES + RING_X * groups - 2
     vmem = pl.BlockSpec(memory_space=pltpu.VMEM)
     flat_out = jax.ShapeDtypeStruct((plan.xs, plan.ys // groups * plan.zs), F32)
     return pl.pallas_call(
-        functools.partial(match_kernel, plan, tiles, groups),
+        functools.partial(match_kernel, plan, tiles, groups, spots),
         out_shape=[flat_out, flat_out, jax.ShapeDtypeStruct((4,) + flat_out.shape, F32)],
         in_specs=[vmem] * 4
         + [pl.BlockSpec(memory_space=pltpu.SMEM)]
@@ -583,7 +596,7 @@
         out_specs=[vmem] * 3,
         scratch_shapes=[
             pltpu.VMEM((2, groups, share, LANES), F32),
-            pltpu.VMEM((groups, RING_X * CORES, ring_z, 1, LANES), F32),
+            pltpu.VMEM((groups, RING_X, ring_z * CORES, 1, LANES), F32),
             pltpu.VMEM(own.shape, BF16),
             pltpu.VMEM(own.shape, BF16),
             pltpu.VMEM((CORES, RING_X, ring_z) + block.shape, BF16),
@@ -601,7 +614,7 @@
             pltpu.SemaphoreType.DMA((2, groups)),
         ],
         compiler_params=pltpu.CompilerParams(
-            collective_id=0, has_side_effects=True, vmem_limit_bytes=60 << 20
+            collective_id=0, has_side_effects=True, vmem_limit_bytes=48 << 20
         ),
         name="match",
     )(own, block, valid, quats, rot_index, *tables)

time: 104 us -> 102 us (0.981)
  Pallas kernels: 97.4 us -> 94.8 us
    pallas_call x1, Pallas kernels: 97.4 us -> 94.8 us  [matched(): pl.pallas_call(functools.partial(match_kernel, plan, tiles, groups, spots...]
    unnamed x6 -> x18, local copies, waits for them, and re-layouts: 4.12 us -> 5 us
where the time goes in v4:
time: 102 us; the launch traced here: 101 us
  Pallas kernels  94.8 us (93%)
  local copies, waits for them, and re-layouts  5.95 us (6%)
    pallas_call x1, Pallas kernels, matched(): pl.pallas_call(functools.partial(match_kernel, plan, tiles, groups, spots...  94.8 us
    unnamed x18, local copies, waits for them, and re-layouts  5 us

profile of v4, /device:TPU:1, one launch (start us, length us, event | category | flops | bytes accessed | tf_op | source)
XLA Modules:
  0.0 101.5 jit_solution(6198795792260717332)
XLA Ops:
  0.6 0.8 reshape.12
  1.5 0.0 copy-start.3
  1.5 0.0 copy-start.2
  1.6 0.1 reshape.13
  1.7 0.0 copy-start.4
  1.7 0.0 copy-start.5
  1.7 0.0 copy-start.6
  1.7 0.6 copy-done.3
  2.3 0.1 copy-done.2
  2.4 0.0 copy-done.4
  2.4 0.0 copy-done.5
  2.4 0.0 copy-done.6
  2.4 0.0 copy-start
  2.4 1.1 %copy-done = bf16[1408,256]{1,0:T(8,128)(2,1)S(1)} copy-done((bf16[1408,256]{1,0:T(8,128)(2,1)S(1)}, bf16[1408,256]{1,0:T(8,128)(2,1)}, u32[]{:S(2)}) %copy-start) | copy-done | bytes 720920
  3.5 0.0 copy-start.1
  3.5 1.0 copy-done.1
  4.5 94.8 %match.1 = (f32[32,1280]{1,0:T(8,128)S(1)}, f32[32,1280]{1,0:T(8,128)S(1)}, f32[4,32,1280]{2,1,0:T(8,128)S(1)}) custom-call(bf16[32,5120]{1,0:T(8,128)(2,1)S(1)} %copy-done.1, bf16[80,128]{1,0:T(8,128)(2,1)S(1)} %pad.9.block, s32[32,80]{1,0:T(8,128)S(1)} %copy-done.4, f32[4,4096]{1,0:T(4,128)S(1)} %copy-done.2, s32[4]{0:T(128)S(1)} %copy-done.6, ...), custom_call_target="tpu_custom_call" | custom-call | tf_op jit(solution)/shard_map/match/pallas_call | solution.py:590
  99.3 0.7 copy.17
  100.0 0.7 copy.18
  100.7 0.8 copy.19
  (3 shorter events, 0.1 us)
Async XLA Ops:
  1.5 0.8 copy-start.3
  1.5 0.8 copy-start.2
  1.7 0.7 copy-start.4
  1.7 0.7 copy-start.5
  1.7 0.7 copy-start.6
  2.4 1.1 %copy-start = (bf16[1408,256]{1,0:T(8,128)(2,1)S(1)}, bf16[1408,256]{1,0:T(8,128)(2,1)}, u32[]{:S(2)}) copy-start(bf16[1408,256]{1,0:T(8,128)(2,1)} %constant.9.clone.packed) | copy-start | bytes 2162692
  3.5 1.0 copy-start.1

commit v5 on v4

--- a/solution.py
+++ b/solution.py
@@ -20,8 +20,9 @@
 BLOCK = 80
 HALO_PARTS = 4
 MESH = pl.DeviceIdType.MESH
-FIELD_COUNT = 4
-FIELD_QUAT = 5
+FIELDS = 4
+FIELD_COUNT = 8
+FIELD_QUAT = 16
 F32 = jnp.float32
 BF16 = jnp.bfloat16
 
@@ -87,8 +88,7 @@
         sin = np.zeros((ZF, ZF))
         cos[:TEMPL, : self.kz] = np.cos(angle)
         sin[:TEMPL, : self.kz] = np.sin(angle)
-        none = np.zeros_like(cos)
-        return np.block([[cos, none, sin, none], [none, cos, none, sin]])
+        return np.kron(np.eye(2), np.concatenate([cos, sin], axis=1))
 
     def inverse_rows(self, points, count, length, k_pad, tail):
         angle = phases(points, np.arange(count), length)
@@ -106,8 +106,7 @@
         weight[self.kz - 1] *= 0.5
         cos = padded_rows(np.cos(angle) * weight, ZF)
         sin = padded_rows(-np.sin(angle) * weight, ZF)
-        none = np.zeros_like(cos)
-        return np.block([[cos, none], [none, cos], [sin, none], [none, sin]])
+        return np.kron(np.eye(2), np.concatenate([cos, sin], axis=0))
 
 
 def unrolled(body, count):
@@ -153,14 +152,6 @@
     count = table.shape[0] // 2
     both = mm(table, jnp.concatenate([high, low], axis=0))
     return both[:count] + both[count:]
-
-
-def plus_minus(folded, count, sign):
-    cos_re, cos_im = folded[:count, :LANES], folded[:count, LANES:]
-    sin_re, sin_im = folded[count:, :LANES], folded[count:, LANES:]
-    first = (cos_re - sin_im, cos_im + sin_re)
-    second = (cos_re + sin_im, cos_im - sin_re)
-    return (first, second) if sign > 0 else (second, first)
 
 
 def exact(left, right):
@@ -271,17 +262,17 @@
 
     flags = valid[...].astype(F32)
     columns = jnp.sum(flags)
-    for y in range(ys):
-        marks[y * xs : y * xs + xs, :] = jnp.broadcast_to(flags[:, y : y + 1], (xs, LANES))
-    field = lax.rem(lax.broadcasted_iota(jnp.int32, (1, LANES), 1), ZF)
+    for y in range(0, ys, 2):
+        marks[y // 2 * xs : y // 2 * xs + xs, :] = jnp.where(
+            low_half, flags[:, y : y + 1], flags[:, y + 1 : y + 2]
+        )
+    field = lax.broadcasted_iota(jnp.int32, (1, LANES), 1)
     line = jnp.where(field == FIELD_COUNT, columns, 0.0)
     entry = lax.broadcasted_iota(jnp.int32, quats.shape, 1)
-    for r in range(4):
+    for r in range(FIELDS):
         found = jnp.sum(jnp.where(entry == rot_index[r], quats[...], 0.0), axis=1, keepdims=True)
-        half = low_half if r % 2 == 0 else jnp.logical_not(low_half)
         for c in range(4):
-            here = jnp.logical_and(field == FIELD_QUAT + 4 * (r // 2) + c, half)
-            line = jnp.where(here, found[c : c + 1], line)
+            line = jnp.where(field == FIELD_QUAT + 4 * r + c, found[c : c + 1], line)
     row[...] = line
 
     def slab_first(j, carry):
@@ -328,7 +319,7 @@
             for u in range(2):
                 swapped = pltpu.roll(sides[u], ZF, 1)
                 spectrum[k, s, u, :, :LANES] = jnp.where(low_half, sides[u], swapped)
-                spectrum[k, s, u, :, LANES:] = jnp.where(low_half, swapped, sides[u])
+                spectrum[k, s, u, :, LANES:] = jnp.where(low_half, -swapped, sides[u])
         return carry
 
     trips = plan.kxc // 11
@@ -379,7 +370,16 @@
     factors = [
         1.0 / (jnp.sqrt(square / total + EPSILON) * float(TEMPL) ** 1.5) for square in squares
     ]
-    scale_rows = jnp.where(place < per, factors[0], factors[1])[None]
+    scale_rows = jnp.where(place < per, factors[0], factors[1])
+
+    def for_halves(value):
+        swapped = pltpu.roll(value, ZF, 1)
+        return (
+            jnp.where(low_half, value, swapped)[None],
+            jnp.where(low_half, swapped, value)[None],
+        )
+
+    mean_halves, scale_halves = for_halves(mean_rows[0]), for_halves(scale_rows)
 
     def z_stage(i, carry):
         lines = bank_rows(i).reshape(tall, LANES)
@@ -388,109 +388,126 @@
         for part in range(2):
             lanes = slice(part * LANES, part * LANES + LANES)
             side = value[:, lanes].reshape(ring_z, BLOCK, LANES)
-            side = (side - mean_rows * zsum[:, lanes]) * scale_rows
+            side = (side - mean_halves[part] * zsum[:, lanes]) * scale_halves[part]
             zed[part, at, :] = side.reshape(tall, LANES)
         return carry
 
     lax.fori_loop(0, plane_size, z_stage, 0)
     share = ys // groups
-    step = share
-
-    def pair(p, outer):
-        def x_stage(b, carry):
-            lines = []
+    lines_out = share // 2 * xs
+    piece = per // 3
+    upper_sign = jnp.where(low_half, 1.0, -1.0)
+
+    def one(q, outer):
+        p, h = q // 2, lax.rem(q, 2)
+
+        def x_stage(g, carry):
+            starts = []
             for s in range(TEMPL // ring_z):
-                index = s * TEMPL + b
-                owner = index // per
+                m = s * (TEMPL // piece) + g
+                owner = m // 3
                 there = lax.rem(owner, CORES) * RING_X + owner // CORES
-                at = pl.ds(there * tall + p * per + lax.rem(index, per), ring_z, stride=BLOCK)
-                lines.append(jnp.concatenate([zed[0, at, :], zed[1, at, :]], axis=1))
-            folded = stacked_product(table_x[...], jnp.concatenate(lines, axis=0))
-            for s, (re, im) in enumerate(plus_minus(folded, kxp, 1)):
-                to = pl.ds(pl.multiple_of(b * rows + s * kxp, 8), kxp)
-                mid[0, to, :] = re
-                mid[1, to, :] = im
+                starts.append(there * tall + p * per + lax.rem(m, 3) * piece)
+
+            def column(t):
+                lines = [zed[h, pl.ds(at + t, ring_z, stride=BLOCK), :] for at in starts]
+                return jnp.concatenate(lines, axis=0)
+
+            for t in range(0, piece, 2):
+                value = jnp.concatenate([column(t), column(t + 1)], axis=1)
+                folded = stacked_product(table_x[...], value)
+                for part in range(2):
+                    lanes = slice(part * LANES, part * LANES + LANES)
+                    first, second = packed_sides(folded[:, lanes], kxp, low_half)
+                    to = pl.multiple_of((g * piece + t + part) * rows, 8)
+                    mid[pl.ds(to, kxp), :] = second
+                    mid[pl.ds(pl.multiple_of(to + kxp, 8), kxp), :] = first
             return carry
 
-        lax.fori_loop(0, TEMPL // 12, unrolled(x_stage, 12), 0)
+        lax.fori_loop(0, TEMPL // piece, x_stage, 0)
 
         def y_stage(k, carry):
-            found = []
+            lines = [mid[pl.ds(k + s * kxp, TEMPL, stride=rows), :] for s in range(2)]
+            folded = stacked_product(table_y[...], jnp.concatenate(lines, axis=1))
+            evens, odds = [], []
             for s in range(2):
-                at = pl.ds(k + s * kxp, TEMPL, stride=rows)
-                value = jnp.concatenate([mid[0, at, :], mid[1, at, :]], axis=1)
-                folded = stacked_product(table_y[...], value)
-                sides = []
-                for u, (re, im) in enumerate(plus_minus(folded, kyp, 1)):
-                    slab_re = spectrum[k, s, u, :, :LANES]
-                    slab_im = spectrum[k, s, u, :, LANES:]
-                    sides.append((re * slab_re - im * slab_im, re * slab_im + im * slab_re))
-                (re_p, im_p), (re_m, im_m) = sides
-                even = jnp.concatenate([re_p + re_m, im_p + im_m], axis=1)
-                odd = jnp.concatenate([im_m - im_p, re_p - re_m], axis=1)
-                found.append(paired_product(table_yi[...], jnp.concatenate([even, odd], axis=0)))
-            even = found[0] + found[1]
-            odd = found[0] - found[1]
-            to = pl.ds(pl.multiple_of(k * ys, 8), ys)
-            back[0, to, :] = even[:, :LANES]
-            back[1, to, :] = even[:, LANES:]
-            to = pl.ds(pl.multiple_of((k + plan.kxc) * ys, 8), ys)
-            back[0, to, :] = -odd[:, LANES:]
-            back[1, to, :] = odd[:, :LANES]
+                lanes = slice(s * LANES, s * LANES + LANES)
+                cos, sin = folded[:kyp, lanes], folded[kyp:, lanes]
+                cos_turned, sin_turned = pltpu.roll(cos, ZF, 1), pltpu.roll(sin, ZF, 1)
+                side = -upper_sign * sin_turned
+                side_turned = upper_sign * sin
+                found = []
+                for u in range(2):
+                    value = cos + side if u == 0 else cos - side
+                    turned = cos_turned + side_turned if u == 0 else cos_turned - side_turned
+                    found.append(
+                        value * spectrum[k, s, u, :, :LANES] + turned * spectrum[k, s, u, :, LANES:]
+                    )
+                evens.append(found[0] + found[1])
+                odds.append(-upper_sign * pltpu.roll(found[0] - found[1], ZF, 1))
+            stacked = jnp.concatenate(
+                [jnp.concatenate(evens, axis=1), jnp.concatenate(odds, axis=1)], axis=0
+            )
+            result = paired_product(table_yi[...], stacked)
+            first, second = result[:, :LANES], result[:, LANES:]
+            back[pl.ds(pl.multiple_of(k * ys, 8), ys), :] = first + second
+            odd = -upper_sign * pltpu.roll(first - second, ZF, 1)
+            back[pl.ds(pl.multiple_of((k + plan.kxc) * ys, 8), ys), :] = odd
             return carry
 
-        lax.fori_loop(0, plan.kxc // 11, unrolled(y_stage, 11), 0)
+        lax.fori_loop(0, plan.kxc // 22, unrolled(y_stage, 22), 0)
 
         def last(i, lane_sum):
             j = lax.rem(2 + 3 * i + 3 * (i * (i - 1) // 2), groups)
             base = lax.rem(rot + j, groups) * share
             lines = []
-            for y in range(step):
-                at = pl.ds(base + y, plan.kxi, stride=ys)
-                value = jnp.concatenate([back[0, at, :], back[1, at, :]], axis=1)
+            for y in range(0, share, 2):
+                value = jnp.concatenate(
+                    [back[pl.ds(base + y + part, plan.kxi, stride=ys), :] for part in range(2)],
+                    axis=1,
+                )
                 lines.append(rows_product(table_xi[...], value))
             upper, lower = split(jnp.concatenate(lines, axis=0))
             both = mm(upper, table_zi[...])
             value = both[:, :LANES] + both[:, LANES:] + mm(lower, table_zi[:, :LANES])
-            ready[p, j] = value
+            ready[q, j] = value
 
             @pl.when(j > 0)
             def _():
-                send_part(p, j).start()
-
-            mark = marks[pl.ds(pl.multiple_of(base * xs, 8), share * xs), :]
+                send_part(q, j).start()
+
+            mark = marks[pl.ds(pl.multiple_of(base // 2 * xs, 8), lines_out), :]
             return lane_sum + tall_sum(value * mark)
 
-        def send_part(p, j):
+        def send_part(q, j):
             return pltpu.make_async_remote_copy(
-                src_ref=ready.at[p, j],
-                dst_ref=parts.at[p, j],
-                send_sem=part_sends.at[p, j],
-                recv_sem=part_receives.at[p, j],
+                src_ref=ready.at[q, j],
+                dst_ref=parts.at[q, j],
+                send_sem=part_sends.at[q, j],
+                recv_sem=part_receives.at[q, j],
                 device_id={"rot": lax.rem(rot + j, groups)},
                 device_id_type=MESH,
             )
 
+        def sum_all(value):
+            return jnp.sum(jnp.sum(value, axis=0, keepdims=True), axis=1, keepdims=True)
+
+        cells = columns * float(plan.zs)
         lane_sum = lax.fori_loop(0, groups, last, jnp.zeros((8, LANES), F32))
-        lane_mean = jnp.sum(lane_sum, axis=0, keepdims=True) / jnp.maximum(columns, 1.0)
+        part_mean = sum_all(lane_sum) / jnp.maximum(cells, 1.0)
 
         def add_off(j, carry):
-            base = lax.rem(rot + j, groups) * (share * xs)
-            mark = marks[pl.ds(pl.multiple_of(base, 8), share * xs), :]
-            off = ready[p, j] - lane_mean
+            base = lax.rem(rot + j, groups) * lines_out
+            mark = marks[pl.ds(pl.multiple_of(base, 8), lines_out), :]
+            off = ready[q, j] - part_mean
             return carry + tall_sum(off * off * mark)
 
-        lane_square = lax.fori_loop(0, groups, add_off, jnp.zeros((8, LANES), F32))
-        wide = jnp.broadcast_to(lane_mean, (8, LANES))
-        part_mean = exact(wide, ones[...])[:1] / float(plan.zs)
-        off = lane_mean - part_mean
-        lane_square = jnp.sum(lane_square, axis=0, keepdims=True) + columns * off * off
-        part_square = exact(jnp.broadcast_to(lane_square, (8, LANES)), ones[...])[:1]
-        now = jnp.where(field == 2 * p, part_mean, row[...])
-        row[...] = jnp.where(field == 2 * p + 1, part_square, now)
+        part_square = sum_all(lax.fori_loop(0, groups, add_off, jnp.zeros((8, LANES), F32)))
+        now = jnp.where(field == q, part_mean, row[...])
+        row[...] = jnp.where(field == FIELDS + q, part_square, now)
         return outer
 
-    lax.fori_loop(0, 2, pair, 0)
+    lax.fori_loop(0, FIELDS, one, 0)
     place = z * CORES + core
     stats[rot, x, place] = row[...]
     mine = stats.at[rot, x, place]
@@ -499,14 +516,9 @@
     finish(begin(mine, mine, sends, receives, first_stats + line_size - 1, sheet_peers))
     incoming = [
         remote(ready.at[p, j], parts.at[p, j], part_sends.at[p], part_receives.at[p], j, {"rot": lax.rem(rot + j, groups)})
-        for p in range(2)
+        for p in range(FIELDS)
         for j in range(1, groups)
     ]
-
-    def spread_field(lines, index):
-        return jnp.where(
-            low_half, lines[:, index : index + 1], lines[:, ZF + index : ZF + index + 1]
-        )
 
     terms = []
     for j in range(groups):
@@ -517,41 +529,30 @@
         average = jnp.sum(count * lines, axis=0, keepdims=True) / total
         off = lines - average
         square = jnp.sum(count * off * off, axis=0, keepdims=True) * plan.zs
-        square += pltpu.roll(jnp.sum(lines, axis=0, keepdims=True), LANES - 1, 1)
+        square += pltpu.roll(jnp.sum(lines, axis=0, keepdims=True), LANES - FIELDS, 1)
         inverse = 1.0 / jnp.sqrt(square / (total * plan.zs) + EPSILON)
-        for p in range(2):
+        for q in range(FIELDS):
             source = ready if j == 0 else parts
-            quat = [spread_field(lines[:1], FIELD_QUAT + 4 * p + c) for c in range(4)]
-            terms.append(
-                (source.at[p, j], spread_field(average, 2 * p), spread_field(inverse, 2 * p), quat)
-            )
+            at = FIELD_QUAT + 4 * q
+            quat = [lines[:1, at + c : at + c + 1] for c in range(4)]
+            terms.append((source.at[q, j], average[:, q : q + 1], inverse[:, q : q + 1], quat))
 
     finish(incoming)
 
-    def column(y):
-        at = pl.ds(pl.multiple_of(y * xs, 8), xs)
+    def answer(j, carry):
+        at = pl.ds(pl.multiple_of(j * xs, 8), xs)
         scores = [(ref[at, :] - average) * inverse for ref, average, inverse, _ in terms]
         high = functools.reduce(jnp.maximum, scores)
-        high = jnp.maximum(high, pltpu.roll(high, ZF, 1))
         weights = [jnp.exp(score - high) for score in scores]
-        sums = [functools.reduce(jnp.add, weights)]
-        for c in range(4):
-            sums.append(functools.reduce(jnp.add, [w * t[3][c] for w, t in zip(weights, terms)]))
-        return [high] + [value + pltpu.roll(value, ZF, 1) for value in sums]
-
-    def answer(j, carry):
-        both = [jnp.where(low_half, a, b) for a, b in zip(column(2 * j), column(2 * j + 1))]
-        base = pl.multiple_of(rot * (share * xs) + 2 * j * xs, 8)
-        inside = jnp.where(
-            low_half, marks[pl.ds(base, xs), :], marks[pl.ds(pl.multiple_of(base + xs, 8), xs), :]
-        )
-        high, total = both[0], both[1]
+        total = functools.reduce(jnp.add, weights)
+        inside = marks[pl.ds(pl.multiple_of(rot * lines_out + j * xs, 8), xs), :]
         lanes = pl.ds(pl.multiple_of(j * LANES, LANES), LANES)
         best[:, lanes] = inside * high
         evidence[:, lanes] = inside * (high + jnp.log(total))
         ratio = inside / total
         for c in range(4):
-            moments[c, :, lanes] = both[2 + c] * ratio
+            moment = functools.reduce(jnp.add, [w * t[3][c] for w, t in zip(weights, terms)])
+            moments[c, :, lanes] = moment * ratio
         return carry
 
     lax.fori_loop(0, share // 2 // 5, unrolled(answer, 5), 0)
@@ -595,7 +596,7 @@
         + [vmem] * len(tables),
         out_specs=[vmem] * 3,
         scratch_shapes=[
-            pltpu.VMEM((2, groups, share, LANES), F32),
+            pltpu.VMEM((FIELDS, groups, share // 2, LANES), F32),
             pltpu.VMEM((groups, RING_X, ring_z * CORES, 1, LANES), F32),
             pltpu.VMEM(own.shape, BF16),
             pltpu.VMEM(own.shape, BF16),
@@ -603,15 +604,15 @@
             pltpu.VMEM((plan.kxc, 2, 2, plan.kyp, 2 * LANES), F32),
             pltpu.VMEM((plan.ys * 2 * plan.kxp, LANES), F32),
             pltpu.VMEM((2, tiles * BLOCK, LANES), F32),
-            pltpu.VMEM((2, TEMPL * 2 * plan.kxp, LANES), F32),
-            pltpu.VMEM((2, plan.kxi * plan.ys, LANES), F32),
-            pltpu.VMEM((plan.ys * plan.xs, LANES), F32),
-            pltpu.VMEM((2, groups, share, LANES), F32),
+            pltpu.VMEM((TEMPL * 2 * plan.kxp, LANES), F32),
+            pltpu.VMEM((plan.kxi * plan.ys, LANES), F32),
+            pltpu.VMEM((plan.ys // 2 * plan.xs, LANES), F32),
+            pltpu.VMEM((FIELDS, groups, share // 2, LANES), F32),
             pltpu.VMEM((1, LANES), F32),
             pltpu.SemaphoreType.DMA((copies,)),
             pltpu.SemaphoreType.DMA((copies,)),
-            pltpu.SemaphoreType.DMA((2, groups)),
-            pltpu.SemaphoreType.DMA((2, groups)),
+            pltpu.SemaphoreType.DMA((FIELDS, groups)),
+            pltpu.SemaphoreType.DMA((FIELDS, groups)),
         ],
         compiler_params=pltpu.CompilerParams(
             collective_id=0, has_side_effects=True, vmem_limit_bytes=48 << 20

time: 102 us -> 109 us (1.069)
  Pallas kernels: 94.8 us -> 102 us
    pallas_call x1, Pallas kernels: 94.8 us -> 102 us  [matched(): pl.pallas_call(functools.partial(match_kernel, plan, tiles, groups, spots...]
where the time goes in v5:
time: 109 us; the launch traced here: 108 us
  Pallas kernels  102 us (94%)
  local copies, waits for them, and re-layouts  5.95 us (5%)
    pallas_call x1, Pallas kernels, matched(): pl.pallas_call(functools.partial(match_kernel, plan, tiles, groups, spots...  102 us
    unnamed x18, local copies, waits for them, and re-layouts  5 us

profile of v5, /device:TPU:1, one launch (start us, length us, event | category | flops | bytes accessed | tf_op | source)
XLA Modules:
  0.0 108.5 jit_solution(2561703271320202921)
XLA Ops:
  0.6 0.8 reshape.12
  1.5 0.0 copy-start.3
  1.5 0.0 copy-start.2
  1.6 0.1 reshape.13
  1.7 0.0 copy-start.4
  1.7 0.0 copy-start.5
  1.7 0.0 copy-start.6
  1.7 0.6 copy-done.3
  2.3 0.1 copy-done.2
  2.4 0.0 copy-done.4
  2.4 0.0 copy-done.5
  2.4 0.0 copy-done.6
  2.4 0.0 copy-start
  2.4 1.1 %copy-done = bf16[1408,256]{1,0:T(8,128)(2,1)S(1)} copy-done((bf16[1408,256]{1,0:T(8,128)(2,1)S(1)}, bf16[1408,256]{1,0:T(8,128)(2,1)}, u32[]{:S(2)}) %copy-start) | copy-done | bytes 720920
  3.5 0.0 copy-start.1
  3.5 1.0 copy-done.1
  4.5 101.8 %match.1 = (f32[32,1280]{1,0:T(8,128)S(1)}, f32[32,1280]{1,0:T(8,128)S(1)}, f32[4,32,1280]{2,1,0:T(8,128)S(1)}) custom-call(bf16[32,5120]{1,0:T(8,128)(2,1)S(1)} %copy-done.1, bf16[80,128]{1,0:T(8,128)(2,1)S(1)} %pad.9.block, s32[32,80]{1,0:T(8,128)S(1)} %copy-done.4, f32[4,4096]{1,0:T(4,128)S(1)} %copy-done.2, s32[4]{0:T(128)S(1)} %copy-done.6, ...), custom_call_target="tpu_custom_call" | custom-call | tf_op jit(solution)/shard_map/match/pallas_call | solution.py:591
  106.3 0.7 copy.17
  107.0 0.7 copy.18
  107.7 0.8 copy.19
  (3 shorter events, 0.1 us)
Async XLA Ops:
  1.5 0.8 copy-start.3
  1.5 0.8 copy-start.2
  1.7 0.7 copy-start.4
  1.7 0.7 copy-start.5
  1.7 0.7 copy-start.6
  2.4 1.1 %copy-start = (bf16[1408,256]{1,0:T(8,128)(2,1)S(1)}, bf16[1408,256]{1,0:T(8,128)(2,1)}, u32[]{:S(2)}) copy-start(bf16[1408,256]{1,0:T(8,128)(2,1)} %constant.9.clone.packed) | copy-start | bytes 2162692
  3.5 1.0 copy-start.1

commit v6 on v4

--- a/solution.py
+++ b/solution.py
@@ -65,6 +65,7 @@
         self.lx, self.ly, self.lz = xs + TEMPL, ys + HALF, zs + HALF
         self.kx, self.ky, self.kz = self.lx // 2 + 1, self.ly // 2 + 1, self.lz // 2 + 1
         self.kxp, self.kyp = up8(self.kx), up8(self.ky)
+        self.kxu = -(-self.kx // 2) * 2
         self.kxc = -(-self.kx // 4) * 4
         self.kxi = 2 * self.kxc
 
@@ -253,6 +254,10 @@
     first_pass = first_x + RING_X
     first_stats = first_pass + RING_X - 1
 
+    for k in range(plan.kxu, plan.kxc):
+        for side in range(2):
+            first = (k + side * plan.kxc) * ys
+            back[:, first : first + ys, :] = jnp.zeros((2, ys, LANES), F32)
     greet([after, before] + line_peers + sheet_peers)
 
     def halo(q):
@@ -284,22 +289,26 @@
             line = jnp.where(here, found[c : c + 1], line)
     row[...] = line
 
-    def slab_first(j, carry):
-        lanes = pl.ds(pl.multiple_of(j * LANES, LANES), LANES)
-        strips = [
-            jnp.where(tile > 0, low[:, lanes].astype(F32)[xs - HALF :], 0.0),
-            own[:, lanes].astype(F32),
-            jnp.where(tile < tiles - 1, high[:, lanes].astype(F32)[:HALF], 0.0),
-        ]
-        strip = jnp.concatenate(strips, axis=0).astype(BF16)
-        strip = mm(jnp.concatenate([strip, strip], axis=1), slab_z[...])
-        folded = stacked_product(slab_x[...], strip)
-        for part in range(2):
-            sides = packed_sides(folded[:, part * LANES : part * LANES + LANES], kxp, low_half)
-            for s in range(2):
-                at = pl.ds(pl.multiple_of((2 * j + part) * rows + s * kxp, 8), kxp)
-                slab_mid[at, :] = sides[s]
-        return carry
+    several = 5
+
+    def slab_first(first):
+        blocks = []
+        for t in range(several):
+            lanes = pl.ds(pl.multiple_of((first + t) * LANES, LANES), LANES)
+            blocks += [
+                jnp.where(tile > 0, low[:, lanes].astype(F32)[xs - HALF :], 0.0),
+                own[:, lanes].astype(F32),
+                jnp.where(tile < tiles - 1, high[:, lanes].astype(F32)[:HALF], 0.0),
+            ]
+        block = jnp.concatenate(blocks, axis=0).astype(BF16)
+        strips = mm(jnp.concatenate([block, block], axis=1), slab_z[...])
+        for t in range(several):
+            folded = stacked_product(slab_x[...], strips[t * plan.lx : t * plan.lx + plan.lx])
+            for part in range(2):
+                sides = packed_sides(folded[:, part * LANES : part * LANES + LANES], kxp, low_half)
+                to = pl.multiple_of((2 * (first + t) + part) * rows, 8)
+                for s in range(2):
+                    slab_mid[pl.ds(pl.multiple_of(to + s * kxp, 8), kxp), :] = sides[s]
 
     pieces = ys // 2 // HALO_PARTS
 
@@ -308,11 +317,10 @@
             copy.wait()
 
         def body(i, inner):
-            return lax.fori_loop(
-                0, 5, lambda t, c: slab_first(q * pieces + i * 5 + t, c), inner, unroll=True
-            )
-
-        return lax.fori_loop(0, pieces // 5, body, carry)
+            slab_first(q * pieces + i * several)
+            return inner
+
+        return lax.fori_loop(0, pieces // several, body, carry)
 
     lax.fori_loop(0, HALO_PARTS // 2, slab_part, 0)
     finish(copies)
@@ -324,15 +332,21 @@
         lines = [slab_mid[pl.ds(k + s * kxp, ys, stride=rows), :] for s in range(2)]
         folded = stacked_product(slab_y[...], jnp.concatenate(lines, axis=1))
         for s in range(2):
-            sides = packed_sides(folded[:, s * LANES : s * LANES + LANES], kyp, low_half)
+            lanes = slice(s * LANES, s * LANES + LANES)
+            cos, sin = folded[:kyp, lanes], folded[kyp:, lanes]
+            cos_turned, sin_turned = pltpu.roll(cos, ZF, 1), pltpu.roll(sin, ZF, 1)
             for u in range(2):
-                swapped = pltpu.roll(sides[u], ZF, 1)
-                spectrum[k, s, u, :, :LANES] = jnp.where(low_half, sides[u], swapped)
-                spectrum[k, s, u, :, LANES:] = jnp.where(low_half, swapped, sides[u])
+                re_low, im_high = cos + sin_turned, cos - sin_turned
+                im_low, re_high = cos_turned - sin, cos_turned + sin
+                if u == 1:
+                    re_low, im_high = im_high, re_low
+                    im_low, re_high = re_high, im_low
+                spectrum[k, s, u, :, :LANES] = jnp.where(low_half, re_low, re_high)
+                spectrum[k, s, u, :, LANES:] = jnp.where(low_half, im_low, im_high)
         return carry
 
-    trips = plan.kxc // 11
-    lax.fori_loop(0, trips // 2, unrolled(slab_second, 11), 0)
+    trips = plan.kxu // 21
+    lax.fori_loop(0, trips // 2, unrolled(slab_second, 21), 0)
     forwards = []
     for d in range(1, RING_X):
         copies[d - 1].wait()
@@ -340,7 +354,7 @@
         forward = remote(mine, mine, sends, receives, first_pass + d - 1, other)
         forward.start()
         forwards.append(forward)
-    lax.fori_loop(trips // 2, trips, unrolled(slab_second, 11), 0)
+    lax.fori_loop(trips // 2, trips, unrolled(slab_second, 21), 0)
     copies[-1].wait()
     finish(forwards)
 
@@ -395,24 +409,30 @@
     lax.fori_loop(0, plane_size, z_stage, 0)
     share = ys // groups
     step = share
+    piece = per // 3
 
     def pair(p, outer):
-        def x_stage(b, carry):
-            lines = []
+        def x_stage(g, carry):
+            starts = []
             for s in range(TEMPL // ring_z):
-                index = s * TEMPL + b
-                owner = index // per
+                m = s * (TEMPL // piece) + g
+                owner = m // 3
                 there = lax.rem(owner, CORES) * RING_X + owner // CORES
-                at = pl.ds(there * tall + p * per + lax.rem(index, per), ring_z, stride=BLOCK)
-                lines.append(jnp.concatenate([zed[0, at, :], zed[1, at, :]], axis=1))
-            folded = stacked_product(table_x[...], jnp.concatenate(lines, axis=0))
-            for s, (re, im) in enumerate(plus_minus(folded, kxp, 1)):
-                to = pl.ds(pl.multiple_of(b * rows + s * kxp, 8), kxp)
-                mid[0, to, :] = re
-                mid[1, to, :] = im
+                starts.append(there * tall + p * per + lax.rem(m, 3) * piece)
+            for t in range(piece):
+                lines = []
+                for start in starts:
+                    at = pl.ds(start + t, ring_z, stride=BLOCK)
+                    lines.append(jnp.concatenate([zed[0, at, :], zed[1, at, :]], axis=1))
+                folded = stacked_product(table_x[...], jnp.concatenate(lines, axis=0))
+                to = pl.multiple_of((g * piece + t) * rows, 8)
+                for s, (re, im) in enumerate(plus_minus(folded, kxp, 1)):
+                    at = pl.ds(pl.multiple_of(to + s * kxp, 8), kxp)
+                    mid[0, at, :] = re
+                    mid[1, at, :] = im
             return carry
 
-        lax.fori_loop(0, TEMPL // 12, unrolled(x_stage, 12), 0)
+        lax.fori_loop(0, TEMPL // piece, x_stage, 0)
 
         def y_stage(k, carry):
             found = []
@@ -439,7 +459,7 @@
             back[1, to, :] = odd[:, :LANES]
             return carry
 
-        lax.fori_loop(0, plan.kxc // 11, unrolled(y_stage, 11), 0)
+        lax.fori_loop(0, plan.kxu // 14, unrolled(y_stage, 14), 0)
 
         def last(i, lane_sum):
             j = lax.rem(2 + 3 * i + 3 * (i * (i - 1) // 2), groups)

time: 102 us -> 93.9 us (0.921)
  Pallas kernels: 94.8 us -> 87 us
    pallas_call x1, Pallas kernels: 94.8 us -> 87 us  [matched(): pl.pallas_call(functools.partial(match_kernel, plan, tiles, groups, spots...]
where the time goes in v6:
time: 93.9 us; the launch traced here: 93.7 us
  Pallas kernels  87 us (93%)
  local copies, waits for them, and re-layouts  5.95 us (6%)
    pallas_call x1, Pallas kernels, matched(): pl.pallas_call(functools.partial(match_kernel, plan, tiles, groups, spots...  87 us
    unnamed x18, local copies, waits for them, and re-layouts  5 us

profile of v6, /device:TPU:1, one launch (start us, length us, event | category | flops | bytes accessed | tf_op | source)
XLA Modules:
  0.0 93.7 jit_solution(13393311405122170812)
XLA Ops:
  0.6 0.8 reshape.12
  1.5 0.0 copy-start.3
  1.5 0.0 copy-start.2
  1.6 0.1 reshape.13
  1.7 0.0 copy-start.4
  1.7 0.0 copy-start.5
  1.7 0.0 copy-start.6
  1.7 0.6 copy-done.3
  2.3 0.1 copy-done.2
  2.4 0.0 copy-done.4
  2.4 0.0 copy-done.5
  2.4 0.0 copy-done.6
  2.4 0.0 copy-start
  2.4 1.1 %copy-done = bf16[1408,256]{1,0:T(8,128)(2,1)S(1)} copy-done((bf16[1408,256]{1,0:T(8,128)(2,1)S(1)}, bf16[1408,256]{1,0:T(8,128)(2,1)}, u32[]{:S(2)}) %copy-start) | copy-done | bytes 720920
  3.5 0.0 copy-start.1
  3.5 1.0 %copy-done.1 = bf16[32,5120]{1,0:T(8,128)(2,1)S(1)} copy-done((bf16[32,5120]{1,0:T(8,128)(2,1)S(1)}, bf16[32,5120]{1,0:T(8,128)(2,1)}, u32[]{:S(2)}) %copy-start.1) | copy-done | bytes 327704
  4.5 87.0 %match.1 = (f32[32,1280]{1,0:T(8,128)S(1)}, f32[32,1280]{1,0:T(8,128)S(1)}, f32[4,32,1280]{2,1,0:T(8,128)S(1)}) custom-call(bf16[32,5120]{1,0:T(8,128)(2,1)S(1)} %copy-done.1, bf16[80,128]{1,0:T(8,128)(2,1)S(1)} %pad.9.block, s32[32,80]{1,0:T(8,128)S(1)} %copy-done.4, f32[4,4096]{1,0:T(4,128)S(1)} %copy-done.2, s32[4]{0:T(128)S(1)} %copy-done.6, ...), custom_call_target="tpu_custom_call" | custom-call | tf_op jit(solution)/shard_map/match/pallas_call | solution.py:610
  91.5 0.7 copy.17
  92.2 0.7 copy.18
  92.9 0.8 copy.19
  (3 shorter events, 0.1 us)
Async XLA Ops:
  1.5 0.8 copy-start.3
  1.5 0.8 copy-start.2
  1.7 0.7 copy-start.4
  1.7 0.7 copy-start.5
  1.7 0.7 copy-start.6
  2.4 1.1 %copy-start = (bf16[1408,256]{1,0:T(8,128)(2,1)S(1)}, bf16[1408,256]{1,0:T(8,128)(2,1)}, u32[]{:S(2)}) copy-start(bf16[1408,256]{1,0:T(8,128)(2,1)} %constant.9.clone.packed) | copy-start | bytes 2162692
  3.5 1.0 %copy-start.1 = (bf16[32,5120]{1,0:T(8,128)(2,1)S(1)}, bf16[32,5120]{1,0:T(8,128)(2,1)}, u32[]{:S(2)}) copy-start(bf16[32,5120]{1,0:T(8,128)(2,1)} %own.1) | copy-start | bytes 983044

commit v7 on v6

--- a/solution.py
+++ b/solution.py
@@ -219,7 +219,7 @@
 def match_kernel(
     plan, tiles, groups, spots, own, block, valid, quats, rot_index, packed, zsum, ones, best, evidence, moments, parts,
     stats, low, high, bank, spectrum, slab_mid, zed, mid, back, marks, ready, row, sends,
-    receives, part_sends, part_receives,
+    receives, part_sends, part_receives, passing, relay_sends, relay_receives,
 ):
     slab_z, slab_x, slab_y, table_z, table_x, table_y, table_yi, table_xi, table_zi = [
         packed.at[first : first + tall, :wide] for first, tall, wide in spots
@@ -411,6 +411,21 @@
     step = share
     piece = per // 3
 
+    middle = share * xs // 2
+    across, back_one = {"rot": lax.rem(rot + 2, groups)}, {"rot": lax.rem(rot + 3, groups)}
+
+    def direct(p):
+        source, target = ready.at[p, 2, :middle], parts.at[p, 2, :middle]
+        return remote(source, target, part_sends.at[p], part_receives.at[p], 2, across)
+
+    def hop(p):
+        source, target = ready.at[p, 2, middle:], passing.at[p]
+        return remote(source, target, relay_sends.at[p], relay_receives.at[p], 0, back_one)
+
+    def forward_half(p):
+        source, target = passing.at[p], parts.at[p, 2, middle:]
+        return remote(source, target, relay_sends.at[p], relay_receives.at[p], 1, back_one)
+
     def pair(p, outer):
         def x_stage(g, carry):
             starts = []
@@ -433,6 +448,11 @@
             return carry
 
         lax.fori_loop(0, TEMPL // piece, x_stage, 0)
+
+        @pl.when(p == 1)
+        def _():
+            hop(0).wait_recv()
+            forward_half(0).start()
 
         def y_stage(k, carry):
             found = []
@@ -459,7 +479,7 @@
             back[1, to, :] = odd[:, :LANES]
             return carry
 
-        lax.fori_loop(0, plan.kxu // 14, unrolled(y_stage, 14), 0)
+        lax.fori_loop(0, plan.kxu // 21, unrolled(y_stage, 21), 0)
 
         def last(i, lane_sum):
             j = lax.rem(2 + 3 * i + 3 * (i * (i - 1) // 2), groups)
@@ -474,9 +494,14 @@
             value = both[:, :LANES] + both[:, LANES:] + mm(lower, table_zi[:, :LANES])
             ready[p, j] = value
 
-            @pl.when(j > 0)
+            @pl.when(lax.rem(j, 2) == 1)
             def _():
                 send_part(p, j).start()
+
+            @pl.when(j == 2)
+            def _():
+                hop(p).start()
+                direct(p).start()
 
             mark = marks[pl.ds(pl.multiple_of(base * xs, 8), share * xs), :]
             return lane_sum + tall_sum(value * mark)
@@ -516,11 +541,14 @@
     mine = stats.at[rot, x, place]
     finish(begin(mine, mine, sends, receives, first_stats, line_peers))
     mine = stats.at[rot, x]
-    finish(begin(mine, mine, sends, receives, first_stats + line_size - 1, sheet_peers))
+    copies = begin(mine, mine, sends, receives, first_stats + line_size - 1, sheet_peers)
+    hop(1).wait_recv()
+    forward_half(1).start()
+    finish(copies)
     incoming = [
         remote(ready.at[p, j], parts.at[p, j], part_sends.at[p], part_receives.at[p], j, {"rot": lax.rem(rot + j, groups)})
         for p in range(2)
-        for j in range(1, groups)
+        for j in (1, 3)
     ]
 
     def spread_field(lines, index):
@@ -547,6 +575,10 @@
             )
 
     finish(incoming)
+    for p in range(2):
+        direct(p).wait()
+        hop(p).wait_send()
+        forward_half(p).wait()
 
     def column(y):
         at = pl.ds(pl.multiple_of(y * xs, 8), xs)
@@ -632,6 +664,9 @@
             pltpu.SemaphoreType.DMA((copies,)),
             pltpu.SemaphoreType.DMA((2, groups)),
             pltpu.SemaphoreType.DMA((2, groups)),
+            pltpu.VMEM((2, share // 2, LANES), F32),
+            pltpu.SemaphoreType.DMA((2, 2)),
+            pltpu.SemaphoreType.DMA((2, 2)),
         ],
         compiler_params=pltpu.CompilerParams(
             collective_id=0, has_side_effects=True, vmem_limit_bytes=48 << 20

time: 93.9 us -> 96 us (1.022); the launches traced: 93.7 us -> 94.5 us
  no operation moved by 1% of the time
where the time goes in v7:
time: 96 us; the launch traced here: 94.5 us
  Pallas kernels  87.8 us (91%)
  local copies, waits for them, and re-layouts  5.95 us (6%)
    pallas_call x1, Pallas kernels, matched(): pl.pallas_call(functools.partial(match_kernel, plan, tiles, groups, spots...  87.8 us
    unnamed x18, local copies, waits for them, and re-layouts  5 us

profile of v7, /device:TPU:1, one launch (start us, length us, event | category | flops | bytes accessed | tf_op | source)
XLA Modules:
  0.0 94.5 jit_solution(15216889994398300825)
XLA Ops:
  0.6 0.8 reshape.12
  1.5 0.0 copy-start.3
  1.5 0.0 copy-start.2
  1.6 0.1 reshape.13
  1.7 0.0 copy-start.4
  1.7 0.0 copy-start.5
  1.7 0.0 copy-start.6
  1.7 0.6 copy-done.3
  2.3 0.1 copy-done.2
  2.4 0.0 copy-done.4
  2.4 0.0 copy-done.5
  2.4 0.0 copy-done.6
  2.4 0.0 copy-start
  2.4 1.1 %copy-done = bf16[1408,256]{1,0:T(8,128)(2,1)S(1)} copy-done((bf16[1408,256]{1,0:T(8,128)(2,1)S(1)}, bf16[1408,256]{1,0:T(8,128)(2,1)}, u32[]{:S(2)}) %copy-start) | copy-done | bytes 720920
  3.5 0.0 copy-start.1
  3.5 1.0 %copy-done.1 = bf16[32,5120]{1,0:T(8,128)(2,1)S(1)} copy-done((bf16[32,5120]{1,0:T(8,128)(2,1)S(1)}, bf16[32,5120]{1,0:T(8,128)(2,1)}, u32[]{:S(2)}) %copy-start.1) | copy-done | bytes 327704
  4.5 87.8 %match.1 = (f32[32,1280]{1,0:T(8,128)S(1)}, f32[32,1280]{1,0:T(8,128)S(1)}, f32[4,32,1280]{2,1,0:T(8,128)S(1)}) custom-call(bf16[32,5120]{1,0:T(8,128)(2,1)S(1)} %copy-done.1, bf16[80,128]{1,0:T(8,128)(2,1)S(1)} %pad.9.block, s32[32,80]{1,0:T(8,128)S(1)} %copy-done.4, f32[4,4096]{1,0:T(4,128)S(1)} %copy-done.2, s32[4]{0:T(128)S(1)} %copy-done.6, ...), custom_call_target="tpu_custom_call" | custom-call | tf_op jit(solution)/shard_map/match/pallas_call | solution.py:642
  92.3 0.7 copy.17
  93.0 0.7 copy.18
  93.7 0.8 copy.19
  (3 shorter events, 0.1 us)
Async XLA Ops:
  1.5 0.8 copy-start.3
  1.5 0.8 copy-start.2
  1.7 0.7 copy-start.4
  1.7 0.7 copy-start.5
  1.7 0.7 copy-start.6
  2.4 1.1 %copy-start = (bf16[1408,256]{1,0:T(8,128)(2,1)S(1)}, bf16[1408,256]{1,0:T(8,128)(2,1)}, u32[]{:S(2)}) copy-start(bf16[1408,256]{1,0:T(8,128)(2,1)} %constant.9.clone.packed) | copy-start | bytes 2162692
  3.5 1.0 %copy-start.1 = (bf16[32,5120]{1,0:T(8,128)(2,1)S(1)}, bf16[32,5120]{1,0:T(8,128)(2,1)}, u32[]{:S(2)}) copy-start(bf16[32,5120]{1,0:T(8,128)(2,1)} %own.1) | copy-start | bytes 983044

commit v8 on v6

--- a/solution.py
+++ b/solution.py
@@ -254,6 +254,7 @@
     first_pass = first_x + RING_X
     first_stats = first_pass + RING_X - 1
 
+    bank[core, x, z] = block[...]
     for k in range(plan.kxu, plan.kxc):
         for side in range(2):
             first = (k + side * plan.kxc) * ys
@@ -267,12 +268,11 @@
             remote(own.at[:, lanes], high.at[:, lanes], sends, receives, first_halo + 2 * q + 1, before),
         ]
 
+    mine = bank.at[core, x, z]
+    copies = begin(mine, mine, sends, receives, first_z, z_peers)
     for q in range(HALO_PARTS):
         for copy in halo(q):
             copy.start()
-    bank[core, x, z] = block[...]
-    mine = bank.at[core, x, z]
-    copies = begin(mine, mine, sends, receives, first_z, z_peers)
 
     flags = valid[...].astype(F32)
     columns = jnp.sum(flags)
@@ -322,11 +322,10 @@
 
         return lax.fori_loop(0, pieces // several, body, carry)
 
-    lax.fori_loop(0, HALO_PARTS // 2, slab_part, 0)
     finish(copies)
     mine = bank.at[core, x]
     copies = begin(mine, mine, sends, receives, first_x, x_peers + [other])
-    lax.fori_loop(HALO_PARTS // 2, HALO_PARTS, slab_part, 0)
+    lax.fori_loop(0, HALO_PARTS, slab_part, 0)
 
     def slab_second(k, carry):
         lines = [slab_mid[pl.ds(k + s * kxp, ys, stride=rows), :] for s in range(2)]
@@ -459,7 +458,7 @@
             back[1, to, :] = odd[:, :LANES]
             return carry
 
-        lax.fori_loop(0, plan.kxu // 14, unrolled(y_stage, 14), 0)
+        lax.fori_loop(0, plan.kxu // 21, unrolled(y_stage, 21), 0)
 
         def last(i, lane_sum):
             j = lax.rem(2 + 3 * i + 3 * (i * (i - 1) // 2), groups)

time: 93.9 us -> 93.9 us (level)
  no operation moved by 1% of the time
where the time goes in v8:
time: 93.9 us; the launch traced here: 93.7 us
  Pallas kernels  87 us (93%)
  local copies, waits for them, and re-layouts  5.95 us (6%)
    pallas_call x1, Pallas kernels, matched(): pl.pallas_call(functools.partial(match_kernel, plan, tiles, groups, spots...  87 us
    unnamed x18, local copies, waits for them, and re-layouts  5 us

profile of v8, /device:TPU:1, one launch (start us, length us, event | category | flops | bytes accessed | tf_op | source)
XLA Modules:
  0.0 93.7 jit_solution(1355857021458605897)
XLA Ops:
  0.6 0.8 reshape.12
  1.5 0.0 copy-start.3
  1.5 0.0 copy-start.2
  1.6 0.1 reshape.13
  1.7 0.0 copy-start.4
  1.7 0.0 copy-start.5
  1.7 0.0 copy-start.6
  1.7 0.6 copy-done.3
  2.3 0.1 copy-done.2
  2.4 0.0 copy-done.4
  2.4 0.0 copy-done.5
  2.4 0.0 copy-done.6
  2.4 0.0 copy-start
  2.4 1.1 %copy-done = bf16[1408,256]{1,0:T(8,128)(2,1)S(1)} copy-done((bf16[1408,256]{1,0:T(8,128)(2,1)S(1)}, bf16[1408,256]{1,0:T(8,128)(2,1)}, u32[]{:S(2)}) %copy-start) | copy-done | bytes 720920
  3.5 0.0 copy-start.1
  3.5 1.0 %copy-done.1 = bf16[32,5120]{1,0:T(8,128)(2,1)S(1)} copy-done((bf16[32,5120]{1,0:T(8,128)(2,1)S(1)}, bf16[32,5120]{1,0:T(8,128)(2,1)}, u32[]{:S(2)}) %copy-start.1) | copy-done | bytes 327704
  4.5 87.0 %match.1 = (f32[32,1280]{1,0:T(8,128)S(1)}, f32[32,1280]{1,0:T(8,128)S(1)}, f32[4,32,1280]{2,1,0:T(8,128)S(1)}) custom-call(bf16[32,5120]{1,0:T(8,128)(2,1)S(1)} %copy-done.1, bf16[80,128]{1,0:T(8,128)(2,1)S(1)} %pad.9.block, s32[32,80]{1,0:T(8,128)S(1)} %copy-done.4, f32[4,4096]{1,0:T(4,128)S(1)} %copy-done.2, s32[4]{0:T(128)S(1)} %copy-done.6, ...), custom_call_target="tpu_custom_call" | custom-call | tf_op jit(solution)/shard_map/match/pallas_call | solution.py:609
  91.5 0.7 copy.17
  92.2 0.7 copy.18
  92.8 0.8 copy.19
  (3 shorter events, 0.1 us)
Async XLA Ops:
  1.5 0.8 copy-start.3
  1.5 0.8 copy-start.2
  1.7 0.7 copy-start.4
  1.7 0.7 copy-start.5
  1.7 0.7 copy-start.6
  2.4 1.1 %copy-start = (bf16[1408,256]{1,0:T(8,128)(2,1)S(1)}, bf16[1408,256]{1,0:T(8,128)(2,1)}, u32[]{:S(2)}) copy-start(bf16[1408,256]{1,0:T(8,128)(2,1)} %constant.9.clone.packed) | copy-start | bytes 2162692
  3.5 1.0 %copy-start.1 = (bf16[32,5120]{1,0:T(8,128)(2,1)S(1)}, bf16[32,5120]{1,0:T(8,128)(2,1)}, u32[]{:S(2)}) copy-start(bf16[32,5120]{1,0:T(8,128)(2,1)} %own.1) | copy-start | bytes 983044

commit v9 on v8

--- a/solution.py
+++ b/solution.py
@@ -217,10 +217,16 @@
 
 
 def match_kernel(
-    plan, tiles, groups, spots, own, block, valid, quats, rot_index, packed, zsum, ones, best, evidence, moments, parts,
+    plan, tiles, groups, spots, own_far, block, valid, quats, rot_index, packed_far, zsum, ones, best, evidence, moments, parts,
     stats, low, high, bank, spectrum, slab_mid, zed, mid, back, marks, ready, row, sends,
-    receives, part_sends, part_receives,
+    receives, part_sends, part_receives, own, packed, load_sems,
 ):
+    loads = [
+        pltpu.make_async_copy(packed_far, packed, load_sems.at[0]),
+        pltpu.make_async_copy(own_far, own, load_sems.at[1]),
+    ]
+    for load in loads:
+        load.start()
     slab_z, slab_x, slab_y, table_z, table_x, table_y, table_yi, table_xi, table_zi = [
         packed.at[first : first + tall, :wide] for first, tall, wide in spots
     ]
@@ -264,8 +270,8 @@
     def halo(q):
         lanes = pl.ds(pl.multiple_of(q * width, LANES), width)
         return [
-            remote(own.at[:, lanes], low.at[:, lanes], sends, receives, first_halo + 2 * q, after),
-            remote(own.at[:, lanes], high.at[:, lanes], sends, receives, first_halo + 2 * q + 1, before),
+            remote(own_far.at[:, lanes], low.at[:, lanes], sends, receives, first_halo + 2 * q, after),
+            remote(own_far.at[:, lanes], high.at[:, lanes], sends, receives, first_halo + 2 * q + 1, before),
         ]
 
     mine = bank.at[core, x, z]
@@ -288,6 +294,8 @@
             here = jnp.logical_and(field == FIELD_QUAT + 4 * (r // 2) + c, half)
             line = jnp.where(here, found[c : c + 1], line)
     row[...] = line
+    for load in loads:
+        load.wait()
 
     several = 5
 
@@ -605,13 +613,12 @@
     share = plan.ys // groups * plan.xs
     copies = 2 * HALO_PARTS + ring_z + 2 * RING_X - 2 + ring_z * CORES + RING_X * groups - 2
     vmem = pl.BlockSpec(memory_space=pltpu.VMEM)
+    far = pl.BlockSpec(memory_space=pltpu.HBM)
     flat_out = jax.ShapeDtypeStruct((plan.xs, plan.ys // groups * plan.zs), F32)
     return pl.pallas_call(
         functools.partial(match_kernel, plan, tiles, groups, spots),
         out_shape=[flat_out, flat_out, jax.ShapeDtypeStruct((4,) + flat_out.shape, F32)],
-        in_specs=[vmem] * 4
-        + [pl.BlockSpec(memory_space=pltpu.SMEM)]
-        + [vmem] * len(tables),
+        in_specs=[far, vmem, vmem, vmem, pl.BlockSpec(memory_space=pltpu.SMEM), far, vmem, vmem],
         out_specs=[vmem] * 3,
         scratch_shapes=[
             pltpu.VMEM((2, groups, share, LANES), F32),
@@ -631,9 +638,12 @@
             pltpu.SemaphoreType.DMA((copies,)),
             pltpu.SemaphoreType.DMA((2, groups)),
             pltpu.SemaphoreType.DMA((2, groups)),
+            pltpu.VMEM(own.shape, BF16),
+            pltpu.VMEM(tables[0].shape, BF16),
+            pltpu.SemaphoreType.DMA((2,)),
         ],
         compiler_params=pltpu.CompilerParams(
-            collective_id=0, has_side_effects=True, vmem_limit_bytes=48 << 20
+            collective_id=0, has_side_effects=True, vmem_limit_bytes=52 << 20
         ),
         name="match",
     )(own, block, valid, quats, rot_index, *tables)

time: 93.9 us -> 92.7 us (0.987)
  local copies, waits for them, and re-layouts: 5.95 us -> 4.84 us
    unnamed x18 -> x16, local copies, waits for them, and re-layouts: 5 us -> 3.89 us
where the time goes in v9:
time: 92.7 us; the launch traced here: 92.5 us
  Pallas kernels  87 us (94%)
  local copies, waits for them, and re-layouts  4.84 us (5%)
    pallas_call x1, Pallas kernels, matched(): pl.pallas_call(functools.partial(match_kernel, plan, tiles, groups, spots...  87 us
    unnamed x16, local copies, waits for them, and re-layouts  3.89 us

profile of v9, /device:TPU:1, one launch (start us, length us, event | category | flops | bytes accessed | tf_op | source)
XLA Modules:
  0.0 92.5 jit_solution(7441852677865642925)
XLA Ops:
  0.6 0.8 reshape.12
  1.5 0.0 copy-start.2
  1.5 0.0 copy-start.1
  1.6 0.1 reshape.13
  1.7 0.0 copy-start.3
  1.7 0.0 copy-start.4
  1.7 0.0 copy-start.5
  1.7 0.6 copy-done.2
  2.3 0.1 copy-done.1
  2.4 0.0 copy-done.3
  2.4 0.0 copy-done.4
  2.4 0.0 copy-done.5
  2.4 0.0 copy-start
  2.4 1.0 %copy-done = bf16[32,5120]{1,0:T(8,128)(2,1)S(1)} copy-done((bf16[32,5120]{1,0:T(8,128)(2,1)S(1)}, bf16[32,5120]{1,0:T(8,128)(2,1)}, u32[]{:S(2)}) %copy-start) | copy-done | bytes 327704
  3.4 87.0 %match.1 = (f32[32,1280]{1,0:T(8,128)S(1)}, f32[32,1280]{1,0:T(8,128)S(1)}, f32[4,32,1280]{2,1,0:T(8,128)S(1)}) custom-call(bf16[32,5120]{1,0:T(8,128)(2,1)S(1)} %copy-done, bf16[80,128]{1,0:T(8,128)(2,1)S(1)} %pad.9.block, s32[32,80]{1,0:T(8,128)S(1)} %copy-done.3, f32[4,4096]{1,0:T(4,128)S(1)} %copy-done.1, s32[4]{0:T(128)S(1)} %copy-done.5, ...), custom_call_target="tpu_custom_call" | custom-call | tf_op jit(solution)/shard_map/match/pallas_call | solution.py:618
  90.4 0.7 copy.17
  91.0 0.7 copy.18
  91.7 0.8 copy.19
  (3 shorter events, 0.1 us)
Async XLA Ops:
  1.5 0.8 copy-start.2
  1.5 0.8 copy-start.1
  1.7 0.7 copy-start.3
  1.7 0.7 copy-start.4
  1.7 0.7 copy-start.5
  2.4 1.0 %copy-start = (bf16[32,5120]{1,0:T(8,128)(2,1)S(1)}, bf16[32,5120]{1,0:T(8,128)(2,1)}, u32[]{:S(2)}) copy-start(bf16[32,5120]{1,0:T(8,128)(2,1)} %own_far.1) | copy-start | bytes 983044

commit v10 on v9

--- a/solution.py
+++ b/solution.py
@@ -507,7 +507,7 @@
             off = ready[p, j] - lane_mean
             return carry + tall_sum(off * off * mark)
 
-        lane_square = lax.fori_loop(0, groups, add_off, jnp.zeros((8, LANES), F32))
+        lane_square = lax.fori_loop(0, groups, add_off, jnp.zeros((8, LANES), F32), unroll=True)
         wide = jnp.broadcast_to(lane_mean, (8, LANES))
         part_mean = exact(wide, ones[...])[:1] / float(plan.zs)
         off = lane_mean - part_mean
@@ -581,7 +581,7 @@
             moments[c, :, lanes] = both[2 + c] * ratio
         return carry
 
-    lax.fori_loop(0, share // 2 // 5, unrolled(answer, 5), 0)
+    lax.fori_loop(0, share // 2 // 10, unrolled(answer, 10), 0)
 
 
 def matched(plan, tiles, groups, own, block, valid, quats, rot_index):

time: 92.7 us -> 92.7 us (level)
  no operation moved by 1% of the time
where the time goes in v10:
time: 92.7 us; the launch traced here: 92.5 us
  Pallas kernels  86.9 us (94%)
  local copies, waits for them, and re-layouts  4.84 us (5%)
    pallas_call x1, Pallas kernels, matched(): pl.pallas_call(functools.partial(match_kernel, plan, tiles, groups, spots...  86.9 us
    unnamed x16, local copies, waits for them, and re-layouts  3.89 us

profile of v10, /device:TPU:1, one launch (start us, length us, event | category | flops | bytes accessed | tf_op | source)
XLA Modules:
  0.0 92.5 jit_solution(10177428930176506312)
XLA Ops:
  0.6 0.8 reshape.12
  1.5 0.0 copy-start.2
  1.5 0.0 copy-start.1
  1.6 0.1 reshape.13
  1.7 0.0 copy-start.3
  1.7 0.0 copy-start.4
  1.7 0.0 copy-start.5
  1.7 0.6 copy-done.2
  2.3 0.1 copy-done.1
  2.4 0.0 copy-done.3
  2.4 0.0 copy-done.4
  2.4 0.0 copy-done.5
  2.4 0.0 copy-start
  2.4 1.0 %copy-done = bf16[32,5120]{1,0:T(8,128)(2,1)S(1)} copy-done((bf16[32,5120]{1,0:T(8,128)(2,1)S(1)}, bf16[32,5120]{1,0:T(8,128)(2,1)}, u32[]{:S(2)}) %copy-start) | copy-done | bytes 327704
  3.4 86.9 %match.1 = (f32[32,1280]{1,0:T(8,128)S(1)}, f32[32,1280]{1,0:T(8,128)S(1)}, f32[4,32,1280]{2,1,0:T(8,128)S(1)}) custom-call(bf16[32,5120]{1,0:T(8,128)(2,1)S(1)} %copy-done, bf16[80,128]{1,0:T(8,128)(2,1)S(1)} %pad.9.block, s32[32,80]{1,0:T(8,128)S(1)} %copy-done.3, f32[4,4096]{1,0:T(4,128)S(1)} %copy-done.1, s32[4]{0:T(128)S(1)} %copy-done.5, ...), custom_call_target="tpu_custom_call" | custom-call | tf_op jit(solution)/shard_map/match/pallas_call | solution.py:618
  90.3 0.7 copy.17
  91.0 0.7 copy.18
  91.6 0.8 copy.19
  (3 shorter events, 0.1 us)
Async XLA Ops:
  1.5 0.8 copy-start.2
  1.5 0.8 copy-start.1
  1.7 0.7 copy-start.3
  1.7 0.7 copy-start.4
  1.7 0.7 copy-start.5
  2.4 1.0 %copy-start = (bf16[32,5120]{1,0:T(8,128)(2,1)S(1)}, bf16[32,5120]{1,0:T(8,128)(2,1)}, u32[]{:S(2)}) copy-start(bf16[32,5120]{1,0:T(8,128)(2,1)} %own_far.1) | copy-start | bytes 983044
